TPU v7x, 32 devices: a whole 2x2x4 slice. The times are simulated.
32 devices in a mesh: freq: 8 (over z, x), tmpl: 4 (over y, core).
Axes of the slice: x: 2, y: 2, z: 4, core: 2. Of those that a mesh axis runs over, the one named last changes fastest.
Arguments:
- strain: bfloat16 [2, 16, 2097152], P(None, 'tmpl', 'freq'), may hold values from -6 to 6
- fiducial: bfloat16 [2, 16, 2097152], P(None, 'tmpl', 'freq'), may hold values from -6 to 6
- psd: float32 [16, 2097152], P('tmpl', 'freq'), may hold values from 0.25 to 8
- time_shift: float32 [16], P('tmpl'), may hold values from -8 to 8
- phase_shift: float32 [16], P('tmpl'), may hold values from -3.140625 to 3.140625
- bin_blocks: int32 [8, 32], replicated, may hold values from 1 to 128, as said below
- bin_owner: int32 [8, 32], replicated, may hold values from 0 to 7, as said below
Outputs:
- moved: bfloat16 [2, 16, 256, 16384], P(None, 'tmpl', 'freq')
- summary: float32 [6, 16, 256], P(None, 'tmpl', 'freq')
Inputs may be any that keep to these rules, and one draw needn't show every extreme that they name: `bin_owner`: row p lists, in frequency order, the owners of the bins in the frequencies of index p of freq; each row names every owner exactly 4 times. `bin_blocks`: row p holds, in frequency order, the lengths in blocks of the bins in the frequencies of index p of freq; the 4 bins that row p hands to one owner total 2 * 128 blocks, and some bin of each row is 128 blocks long.
All inputs are finite; a program needn't handle non-finite values.
Results may differ from a plain program's by a relative error of at most 0.001.
The roundings to bfloat16 on the way count: a program that leaves them out, or rounds other values in their place, can miss the bound.
Values may be sent and summed in bfloat16 or wider, within the bound.
A program may use at most 128 MiB of HBM per device.

v0:
```python
import math

import jax
import jax.numpy as jnp
from jax import lax
from jax.sharding import PartitionSpec as P

two_pi = 2.0 * math.pi
ratio_scale = 1.0 / 64.0
power_scale = 1.0 / 2048.0


def extended(array, sides, width):
    for axis, dim in sides:
        peers, length = (lax.axis_size(axis), array.shape[dim])
        up = [(i, (i + 1) % peers) for i in range(peers - 1)]
        down = [(j, i) for i, j in up]
        last = lax.slice_in_dim(array, length - width, length, axis=dim)
        initial = lax.slice_in_dim(array, 0, width, axis=dim)
        before = lax.ppermute(last, axis, up)
        after = lax.ppermute(initial, axis, down)
        array = jnp.concatenate([before, array, after], axis=dim)
    return array


def heterodyne(strain, fiducial, weight, time_shift, phase_shift, unit):
    strain_re = strain[0].astype(jnp.float32)
    strain_im = strain[1].astype(jnp.float32)
    fid_re = fiducial[0].astype(jnp.float32)
    fid_im = fiducial[1].astype(jnp.float32)
    angle = (two_pi * time_shift)[:, None] * unit[None, :] + phase_shift[:, None]
    cosine = jnp.cos(angle)
    sine_val = jnp.sin(angle)
    cross_re = strain_re * fid_re + strain_im * fid_im
    cross_im = strain_im * fid_re - strain_re * fid_im
    prod_re = weight * (cross_re * cosine + cross_im * sine_val)
    prod_im = weight * (cross_im * cosine - cross_re * sine_val)
    power = weight * (fid_re * fid_re + fid_im * fid_im)
    return jnp.stack([prod_re, prod_im, power]).astype(jnp.bfloat16)


def slot_tables(bin_blocks, bin_owner):
    count = bin_blocks.shape[1]
    starts = jnp.cumsum(bin_blocks, axis=1) - bin_blocks
    position = jnp.arange(count, dtype=jnp.int32)
    earlier = position[None, :] < position[:, None]
    same = bin_owner[:, :, None] == bin_owner[:, None, :]
    ranks = jnp.sum(jnp.logical_and(same, earlier[None]).astype(jnp.int32), axis=2)
    return (starts, ranks)


def arrange(values, first_block, lengths, most_blocks):
    lead = values.shape[:-1]
    blocks = values.shape[-1] // 128
    tiled = values.reshape((-1, blocks, 128))
    step_ids = jnp.arange(most_blocks, dtype=jnp.int32)
    block_ids = jnp.minimum(first_block[:, None] + step_ids[None, :], blocks - 1)
    picked = jnp.take(tiled, block_ids.reshape(-1), axis=1)
    slot_count = first_block.shape[0]
    picked = picked.reshape((tiled.shape[0], slot_count, most_blocks, 128))
    live = (step_ids[None, :] < lengths[:, None])[:, :, None]
    picked = jnp.where(live, picked, jnp.zeros((), values.dtype))
    return picked.reshape(lead + (slot_count, most_blocks * 128))


def summarize(moved, power_slots, lengths):
    width = moved.shape[-1]
    offset = (
        jnp.arange(width, dtype=jnp.int32).astype(jnp.float32)[None, :]
        + 0.5
        - 64.0 * lengths.astype(jnp.float32)[:, None]
    ) / 128.0
    values = moved.astype(jnp.float32)
    weighted = power_slots[0].astype(jnp.float32)
    plain_sum = jnp.sum(values, axis=-1) * ratio_scale
    slope_sum = jnp.sum(values * offset, axis=-1) * ratio_scale
    power_sum = jnp.sum(weighted, axis=-1) * power_scale
    power_slope = jnp.sum(weighted * offset, axis=-1) * power_scale
    return jnp.concatenate([plain_sum, slope_sum, power_sum[None], power_slope[None]], axis=0)


def pack_blocks(values, block_ids):
    lead = values.shape[:-1]
    blocks = values.shape[-1] // 128
    tiled = values.reshape((-1, blocks, 128))
    picked = jnp.take(tiled, block_ids.reshape(-1), axis=1)
    return picked.reshape(lead + (block_ids.shape[0], block_ids.shape[1] * 128))


def unpack_blocks(received, block_ids, live):
    lead = received.shape[:-2]
    total = received.shape[-2] * received.shape[-1] // 128
    tiled = received.reshape((-1, total, 128))
    picked = jnp.take(tiled, block_ids.reshape(-1), axis=1)
    slot_count = block_ids.shape[0] * block_ids.shape[1]
    most_blocks = block_ids.shape[2]
    picked = picked.reshape((tiled.shape[0], slot_count, most_blocks, 128))
    picked = jnp.where(
        live.reshape(slot_count, most_blocks, 1), picked, jnp.zeros((), received.dtype)
    )
    return picked.reshape(lead + (slot_count, most_blocks * 128))


def local(strain, fiducial, psd, time_shift, phase_shift, bin_blocks, bin_owner):
    n_freq = lax.axis_size("freq")
    self_index = lax.axis_index("freq")
    width_dev = psd.shape[1]
    blocks_dev = width_dev // 128
    bins_dev = bin_blocks.shape[1]
    pair_bins = bins_dev // n_freq
    most_blocks = 2 * blocks_dev // bins_dev
    span = 2 * most_blocks
    padded = extended(psd, (("freq", 1),), 1)
    weight = 1.0 / (0.25 * (padded[:, :-2] + 2.0 * padded[:, 1:-1] + padded[:, 2:]))
    global_index = self_index * width_dev + jnp.arange(width_dev, dtype=jnp.int32)
    unit = global_index.astype(jnp.float32) / (width_dev * n_freq)
    combined = heterodyne(strain, fiducial, weight, time_shift, phase_shift, unit)
    starts, ranks = slot_tables(bin_blocks, bin_owner)
    local_slot = bin_owner[self_index] * pair_bins + ranks[self_index]
    send_first = jnp.zeros((bins_dev,), jnp.int32).at[local_slot].set(starts[self_index])
    send_length = jnp.zeros((bins_dev,), jnp.int32).at[local_slot].set(bin_blocks[self_index])
    source_ids = jnp.broadcast_to(jnp.arange(n_freq, dtype=jnp.int32)[:, None], bin_owner.shape)
    all_lengths = (
        jnp.zeros((n_freq, n_freq, pair_bins), jnp.int32)
        .at[source_ids, bin_owner, ranks]
        .set(bin_blocks)
    )
    mine = lax.dynamic_index_in_dim(all_lengths, self_index, 1, keepdims=False)
    group_length = send_length.reshape(n_freq, pair_bins)
    group_first = send_first.reshape(n_freq, pair_bins)
    group_offset = jnp.cumsum(group_length, axis=1) - group_length
    packed_steps = jnp.arange(span, dtype=jnp.int32)
    which = jnp.sum(
        (group_offset[:, None, 1:] <= packed_steps[None, :, None]).astype(jnp.int32), axis=2
    )
    packed_base = jnp.take_along_axis(group_first - group_offset, which, axis=1)
    packed_ids = packed_base + packed_steps[None, :]
    mine_offset = jnp.cumsum(mine, axis=1) - mine
    slot_steps = jnp.arange(most_blocks, dtype=jnp.int32)
    landing = (jnp.arange(n_freq, dtype=jnp.int32)[:, None] * span + mine_offset)[
        :, :, None
    ] + slot_steps[None, None, :]
    landing = jnp.minimum(landing, n_freq * span - 1)
    landing_live = slot_steps[None, None, :] < mine[:, :, None]
    slot_all = arrange(combined, send_first, send_length, most_blocks)
    local_summary = summarize(slot_all[:2], slot_all[2:], send_length)
    packed_values = pack_blocks(combined[:2], packed_ids)
    got_values = lax.all_to_all(packed_values, "freq", split_axis=2, concat_axis=2, tiled=True)
    moved = unpack_blocks(got_values, landing, landing_live)
    summary = lax.all_to_all(local_summary, "freq", split_axis=2, concat_axis=2, tiled=True)
    return (moved, summary)


def solution(mesh):
    return jax.shard_map(
        local,
        mesh=mesh,
        in_specs=(
            P(None, "tmpl", "freq"),
            P(None, "tmpl", "freq"),
            P("tmpl", "freq"),
            P("tmpl"),
            P("tmpl"),
            P(),
            P(),
        ),
        out_specs=(P(None, "tmpl", "freq", None), P(None, "tmpl", "freq")),
        check_vma=False,
    )
```

profile of v0, /device:TPU:0, one launch (start us, length us, event | category | flops | bytes accessed | tf_op | source)
XLA Modules:
  0.0 433.3 jit_solution(10417809007624814966)
XLA Ops:
  1.4 4.9 %collective-permute-start = (f32[4,1]{1,0:T(4,128)S(1)}, f32[4,1]{1,0:T(4,128)S(1)}, u32[]{:S(2)}, u32[]{:S(2)}) collective-permute-start(f32[4,1]{1,0:T(4,128)S(1)} %get-tuple-element.22), channel_id=1, source_target_pairs={{0,4},{4,8},{8,12},{12,16},{16,20},{20,24},{24,28},{1,5},{5,9},{9,... | collective-permute-start | bytes 56 | tf_op jit(solution)/shard_map/ppermute | solution.py:20
  6.3 1.3 collective-permute-start.1
  14.7 9.1 %gather_fusion.3 = s32[2048]{0:T(1024)S(1)} fusion(s32[8,4]{1,0:T(8,128)S(1)} %get-tuple-element.18, s32[2048]{0:T(1024)S(1)} %bitcast.84), kind=kCustom, calls=%fused_computation.3 | custom fusion | bytes 32768 | tf_op jit(solution)/shard_map/jit(take_along_axis)/gather | solution.py:136
  24.7 46.9 %multiply_bitcast_fusion.1 = (bf16[1,4,262144]{2,1,0:T(4,128)(2,1)S(1)}, bf16[1,4,262144]{2,1,0:T(4,128)(2,1)S(1)}) fusion(f32[4]{0:T(128)S(1)} %copy-done.5, f32[262144]{0:T(1024)S(1)} %convert_multiply_fusion.8, f32[4]{0:T(128)S(1)} %broadcast_multiply_fusion.4, bf16[2,4,262144]{2,1,0:T(4,128)(2,1)} %param.8, bf16[2,4,262144]{2,1,0:T(4,128)(2,1)} %param.7, ...), kind=kLoop, calls=%fused_computation.37 | loop fusion | flops 30408704 | bytes 17825856 | tf_op jit(solution)/shard_map/stack | solution.py:39
  71.6 39.2 %multiply_bitcast_fusion = bf16[1,4,262144]{2,1,0:T(4,128)(2,1)S(1)} fusion(f32[4]{0:T(128)S(1)} %copy-done.5, f32[262144]{0:T(1024)S(1)} %convert_multiply_fusion.8, f32[4]{0:T(128)S(1)} %broadcast_multiply_fusion.4, bf16[2,4,262144]{2,1,0:T(4,128)(2,1)S(1)} %copy-done.1, bf16[2,4,262144]{2,1,0:T(4,128)(2,1)S(1)} %copy-done.2, ...), kind=kLoop, calls=%fused_computation.36 | loop fusion | flops 25165824 | bytes 15728704 | tf_op jit(solution)/shard_map/stack | solution.py:39
  110.9 6.5 %maximum_convert_fusion = bf16[3,4,262144]{2,1,0:T(4,128)(2,1)} fusion(bf16[1,4,262144]{2,1,0:T(4,128)(2,1)S(1)} %get-tuple-element.21, bf16[1,4,262144]{2,1,0:T(4,128)(2,1)S(1)} %multiply_bitcast_fusion, bf16[1,4,262144]{2,1,0:T(4,128)(2,1)S(1)} %get-tuple-element.20), kind=kLoop, calls=%fused_computation.11 | loop fusion | flops 6291456 | bytes 12582912 | tf_op jit(solution)/shard_map/convert_element_type | solution.py:39
  117.4 9.5 %convert_element_type.65 = bf16[12,2048,128]{2,1,0:T(8,128)(2,1)} reshape(bf16[3,4,262144]{2,1,0:T(4,128)(2,1)} %maximum_convert_fusion) | data formatting | bytes 12582912 | tf_op jit(solution)/shard_map/convert_element_type | solution.py:39
  126.9 9.1 %copy.111 = bf16[12,2048,128]{2,0,1:T(8,128)(2,1)} copy(bf16[12,2048,128]{2,1,0:T(8,128)(2,1)} %convert_element_type.65) | data formatting | bytes 12582912 | tf_op jit(solution)/shard_map/convert_element_type | solution.py:39
  136.0 35.4 %gather_fusion.2 = bf16[4096,12,128]{2,1,0:T(8,128)(2,1)} fusion(bf16[12,2048,128]{2,0,1:T(8,128)(2,1)} %copy.111, s32[4096]{0:T(1024)S(1)} %broadcast_clamp_fusion), kind=kCustom, calls=%fused_computation.2 | custom fusion | bytes 25182208 | tf_op jit(solution)/shard_map/jit(_take)/gather | solution.py:58
  171.4 12.5 %select_select_fusion = bf16[12,32,128,128]{3,0,2,1:T(8,128)(2,1)S(1)} fusion(bf16[12,32,128,128]{3,0,2,1:T(8,128)(2,1)} %bitcast.85, pred[32,128]{1,0:T(8,128)(4,1)S(1)} %compare_and_fusion, pred[32,128]{1,0:T(8,128)(4,1)S(1)} %iota_compare_fusion.1), kind=kLoop, calls=%fused_computation.10 | loop fusion | flops 12582912 | bytes 25174016 | tf_op jit(solution)/shard_map/jit(_where)/select_n | solution.py:62
  183.9 4.5 %convert_reduce_fusion.1 = (f32[4,32]{0,1:T(8,128)S(1)}, f32[4,32]{0,1:T(8,128)S(1)}) fusion(bf16[12,32,128,128]{3,0,2,1:T(8,128)(2,1)S(1)} %select_select_fusion, f32[32,128,128]{2,1,0:T(8,128)S(1)} %subtract_multiply_fusion), kind=kLoop, calls=%fused_computation.13 | loop fusion | flops 8388352 | bytes 6292480 | tf_op jit(solution)/shard_map/reduce_sum | solution.py:77
  188.4 3.4 convert_reduce_fusion
  191.7 3.1 slice.63
  195.9 7.0 %all-to-all-start.1 = ((f32[6,4,32]{0,1,2:T(4,128)}), f32[6,4,32]{0,1,2:T(4,128)S(1)}, u32[]{:S(2)}, u32[]{:S(2)}) async-start(f32[6,4,32]{0,1,2:T(4,128)} %copy.116), calls=%async_computation.1 | async-start | bytes 131072 | tf_op jit(solution)/shard_map/all_to_all | solution.py:150
  202.8 7.1 %reshape.457 = bf16[8,2048,128]{2,1,0:T(8,128)(2,1)} reshape(bf16[2,4,262144]{2,1,0:T(4,128)(2,1)} %slice.63) | data formatting | bytes 8388608 | tf_op jit(solution)/shard_map/reshape | solution.py:85
  209.9 6.2 %copy.104 = bf16[8,2048,128]{2,0,1:T(8,128)(2,1)} copy(bf16[8,2048,128]{2,1,0:T(8,128)(2,1)} %reshape.457) | data formatting | bytes 8388608 | tf_op jit(solution)/shard_map/reshape | solution.py:85
  216.1 16.9 %gather_fusion = bf16[2048,8,128]{2,1,0:T(8,128)(2,1)} fusion(bf16[8,2048,128]{2,0,1:T(8,128)(2,1)} %copy.104, s32[2048]{0:T(1024)S(1)} %broadcast_clamp_fusion.2), kind=kCustom, calls=%fused_computation | custom fusion | bytes 8396800 | tf_op jit(solution)/shard_map/jit(_take)/gather | solution.py:86
  233.0 4.7 %copy.105 = bf16[8,2048,128]{2,1,0:T(8,128)(2,1)} copy(bf16[8,2048,128]{2,0,1:T(8,128)(2,1)} %bitcast.89) | data formatting | bytes 8388608 | tf_op jit(solution)/shard_map/jit(_take)/gather | solution.py:86
  237.8 7.3 %gather.27 = bf16[2,4,8,32768]{3,2,1,0:T(8,128)(2,1)} reshape(bf16[8,2048,128]{2,1,0:T(8,128)(2,1)} %copy.105) | data formatting | bytes 8388608 | tf_op jit(solution)/shard_map/jit(_take)/gather | solution.py:86
  245.1 3.0 broadcast_select_fusion
  248.1 5.3 %copy.106 = bf16[2,4,8,32768]{3,1,0,2:T(4,128)(2,1)} copy(bf16[2,4,8,32768]{3,2,1,0:T(8,128)(2,1)S(1)} %broadcast_select_fusion) | data formatting | bytes 8388608 | tf_op jit(solution)/shard_map/jit(_take)/select_n | solution.py:86
  253.3 6.1 %all-to-all-start = ((bf16[2,4,8,32768]{3,1,0,2:T(4,128)(2,1)}), bf16[2,4,8,32768]{3,1,0,2:T(4,128)(2,1)}, u32[]{:S(2)}, u32[]{:S(2)}) async-start(bf16[2,4,8,32768]{3,1,0,2:T(4,128)(2,1)} %copy.106), calls=%async_computation | async-start | bytes 8388608 | tf_op jit(solution)/shard_map/all_to_all | solution.py:148
  259.7 14.9 %scatter_fusion = s32[8,8,4]{1,0,2:T(8,128)S(1)} fusion(s32[8,8,4]{1,0,2:T(8,128)S(1)} %broadcast_in_dim.115, s32[256]{0:T(256)S(1)} %reshape.489, s32[256]{0:T(256)S(1)} %reshape.491), kind=kCustom, calls=%fused_computation.4 | custom fusion | bytes 6144 | tf_op jit(solution)/shard_map/scatter | solution.py:126
  277.2 1.1 copy_bitcast_fusion
  279.1 72.6 %all-to-all-done = bf16[2,4,8,32768]{3,1,0,2:T(4,128)(2,1)} async-done(((bf16[2,4,8,32768]{3,1,0,2:T(4,128)(2,1)}), bf16[2,4,8,32768]{3,1,0,2:T(4,128)(2,1)}, u32[]{:S(2)}, u32[]{:S(2)}) %all-to-all-start) | async-done | bytes 4194336 | tf_op jit(solution)/shard_map/all_to_all | solution.py:148
  351.6 6.5 %copy.107 = bf16[2,4,8,32768]{3,2,1,0:T(8,128)(2,1)} copy(bf16[2,4,8,32768]{3,1,0,2:T(4,128)(2,1)} %all-to-all-done) | data formatting | bytes 8388608 | tf_op jit(solution)/shard_map/all_to_all | solution.py:148
  358.1 7.4 %reshape.458 = bf16[8,2048,128]{2,1,0:T(8,128)(2,1)} reshape(bf16[2,4,8,32768]{3,2,1,0:T(8,128)(2,1)} %copy.107) | data formatting | bytes 8388608 | tf_op jit(solution)/shard_map/reshape | solution.py:93
  365.5 6.2 %copy.109 = bf16[8,2048,128]{2,0,1:T(8,128)(2,1)} copy(bf16[8,2048,128]{2,1,0:T(8,128)(2,1)} %reshape.458) | data formatting | bytes 8388608 | tf_op jit(solution)/shard_map/reshape | solution.py:93
  371.7 31.0 %gather_fusion.1 = bf16[4096,8,128]{2,1,0:T(8,128)(2,1)} fusion(bf16[8,2048,128]{2,0,1:T(8,128)(2,1)} %copy.109, s32[4096]{0:T(1024)S(1)} %broadcast_clamp_fusion.1), kind=kCustom, calls=%fused_computation.1 | custom fusion | bytes 16793600 | tf_op jit(solution)/shard_map/jit(_take)/gather | solution.py:94
  402.7 7.7 %copy.110 = bf16[8,4096,128]{2,1,0:T(8,128)(2,1)} copy(bf16[8,4096,128]{2,0,1:T(8,128)(2,1)} %bitcast.88) | data formatting | bytes 16777216 | tf_op jit(solution)/shard_map/jit(_take)/gather | solution.py:94
  410.4 13.3 %gather.29 = bf16[2,4,32,16384]{3,2,1,0:T(8,128)(2,1)} reshape(bf16[8,4096,128]{2,1,0:T(8,128)(2,1)} %copy.110) | data formatting | bytes 16777216 | tf_op jit(solution)/shard_map/jit(_take)/gather | solution.py:94
  423.6 9.7 %select_select_fusion.1 = bf16[2,4,32,16384]{3,2,1,0:T(8,128)(2,1)} fusion(bf16[2,4,32,16384]{3,2,1,0:T(8,128)(2,1)} %gather.29, pred[32,16384]{1,0:T(8,128)(4,1)S(1)} %get-tuple-element.26, pred[32,16384]{1,0:T(8,128)(4,1)S(1)} %get-tuple-element.27), kind=kLoop, calls=%fused_computation.15 | loop fusion | flops 8388608 | bytes 17825792 | tf_op jit(solution)/shard_map/jit(_where)/select_n | solution.py:98
  (91 shorter events, 13.1 us)
Async XLA Ops:
  1.4 23.3 %collective-permute-start = (f32[4,1]{1,0:T(4,128)S(1)}, f32[4,1]{1,0:T(4,128)S(1)}, u32[]{:S(2)}, u32[]{:S(2)}) collective-permute-start(f32[4,1]{1,0:T(4,128)S(1)} %get-tuple-element.22), channel_id=1, source_target_pairs={{0,4},{4,8},{8,12},{12,16},{16,20},{20,24},{24,28},{1,5},{5,9},{9,... | collective-permute-start | bytes 56 | tf_op jit(solution)/shard_map/ppermute | solution.py:20
  6.3 18.4 %collective-permute-start.1 = (f32[4,1]{1,0:T(4,128)S(1)}, f32[4,1]{1,0:T(4,128)S(1)}, u32[]{:S(2)}, u32[]{:S(2)}) collective-permute-start(f32[4,1]{1,0:T(4,128)S(1)} %get-tuple-element.23), channel_id=1, source_target_pairs={{4,0},{8,4},{12,8},{16,12},{20,16},{24,20},{28,24},{5,1},{9,5},{13... | collective-permute-start | bytes 56 | tf_op jit(solution)/shard_map/ppermute | solution.py:21
  14.7 10.0 %copy-start.5 = (f32[4]{0:T(128)S(1)}, f32[4]{0:T(128)}, u32[]{:S(2)}) copy-start(f32[4]{0:T(128)} %param.11) | copy-start | bytes 52
  24.7 46.9 %copy-start = (f32[4,262144]{1,0:T(4,128)S(1)}, f32[4,262144]{1,0:T(4,128)}, u32[]{:S(2)}) copy-start(f32[4,262144]{1,0:T(4,128)} %param.9) | copy-start | bytes 12582916
  24.7 46.9 %copy-start.1 = (bf16[2,4,262144]{2,1,0:T(4,128)(2,1)S(1)}, bf16[2,4,262144]{2,1,0:T(4,128)(2,1)}, u32[]{:S(2)}) copy-start(bf16[2,4,262144]{2,1,0:T(4,128)(2,1)} %param.8) | copy-start | bytes 12582916
  24.7 46.9 %copy-start.2 = (bf16[2,4,262144]{2,1,0:T(4,128)(2,1)S(1)}, bf16[2,4,262144]{2,1,0:T(4,128)(2,1)}, u32[]{:S(2)}) copy-start(bf16[2,4,262144]{2,1,0:T(4,128)(2,1)} %param.7) | copy-start | bytes 12582916
  183.9 7.9 %slice-start = ((s8[6291456]{0:T(1024)(128)(4,1)}), s8[4194304]{0:T(1024)(128)(4,1)S(1)}, s32[]{:S(2)}) async-start(s8[6291456]{0:T(1024)(128)(4,1)} %bitcast.86), calls=%async_computation.2 | async-start | bytes 8388608
  188.4 3.4 slice-start.1
  195.9 57.5 %all-to-all-start.1 = ((f32[6,4,32]{0,1,2:T(4,128)}), f32[6,4,32]{0,1,2:T(4,128)S(1)}, u32[]{:S(2)}, u32[]{:S(2)}) async-start(f32[6,4,32]{0,1,2:T(4,128)} %copy.116), calls=%async_computation.1 | async-start | bytes 131072 | tf_op jit(solution)/shard_map/all_to_all | solution.py:150
  253.3 6.1 %copy-start.3 = (s32[8,32]{1,0:T(8,128)S(1)}, s32[8,32]{1,0:T(8,128)}, u32[]{:S(2)}) copy-start(s32[8,32]{1,0:T(8,128)} %param.12) | copy-start | bytes 3076
  253.3 6.2 %copy-start.4 = (s32[8,32]{1,0:T(8,128)S(1)}, s32[8,32]{1,0:T(8,128)}, u32[]{:S(2)}) copy-start(s32[8,32]{1,0:T(8,128)} %param.13) | copy-start | bytes 3076
  253.3 98.3 %all-to-all-start = ((bf16[2,4,8,32768]{3,1,0,2:T(4,128)(2,1)}), bf16[2,4,8,32768]{3,1,0,2:T(4,128)(2,1)}, u32[]{:S(2)}, u32[]{:S(2)}) async-start(bf16[2,4,8,32768]{3,1,0,2:T(4,128)(2,1)} %copy.106), calls=%async_computation | async-start | bytes 8388608 | tf_op jit(solution)/shard_map/all_to_all | solution.py:148
where the time goes:
time: 435 us; the launch traced here: 433 us
  local copies, waits for them, and re-layouts  210 us (48%)
  other arithmetic  131 us (30%)
  waiting for transfers between devices  72.6 us (17%)
  starting transfers between devices  19.2 us (4%)
    another operation x2, other arithmetic, heterodyne(): return jnp.stack([prod_re, prod_im, power]).astype(jnp.bfloat16)  86.1 us
    all_to_all x1, waiting for transfers between devices, local(): lax.all_to_all(packed_values, 'freq', split_axis=2, concat_axis=2, tiled=...  72.6 us
    gather x3, local copies, waits for them, and re-layouts, unpack_blocks(): picked = jnp.take(tiled, block_ids.reshape(-1), axis=1)  51.9 us
    gather x1, local copies, waits for them, and re-layouts, arrange(): picked = jnp.take(tiled, block_ids.reshape(-1), axis=1)  35.4 us
    gather x3, local copies, waits for them, and re-layouts, pack_blocks(): picked = jnp.take(tiled, block_ids.reshape(-1), axis=1)  29 us
    convert_element_type x2, local copies, waits for them, and re-layouts, heterodyne(): return jnp.stack([prod_re, prod_im, power]).astype(jnp.bfloat16)  18.6 us
    scatter x1, local copies, waits for them, and re-layouts, local(): all_lengths = jnp.zeros((n_freq, n_freq, pair_bins), jnp.int32).at[source...  14.9 us
    reshape x2, local copies, waits for them, and re-layouts, unpack_blocks(): tiled = received.reshape((-1, total, 128))  13.6 us
  transfers between devices with their start and end apart: 4, of which 1 were waited for; matrix products, arithmetic and copies ran while one was open for 20% of the time, Pallas kernels for 0%

commit v1 on v0

v1 whole, which is shorter than its diff:
```python
import functools
import math

import jax
import jax.numpy as jnp
from jax import lax
from jax.experimental import pallas as pl
from jax.experimental.pallas import tpu as pltpu
from jax.sharding import PartitionSpec as P

two_pi = 2.0 * math.pi
ratio_scale = 1.0 / 64.0
power_scale = 1.0 / 2048.0
LANES = 128
SUB = 32
TABLE = 256


def het_kernel(strain, fid, psd, prev, nxt, halo, cos_t, sin_t, cos_s, sin_s, prod, sums, pad, power):
    rows = psd.shape[0]
    step, last = pl.program_id(0), pl.num_programs(0) - 1
    pad[8 : 8 + rows] = psd[...]
    pad[0:8] = jnp.where(step == 0, halo[0], prev[...])
    pad[8 + rows : 16 + rows] = jnp.where(step == last, halo[1], nxt[...])
    lane = lax.broadcasted_iota(jnp.int32, (SUB, LANES), 1)
    fold = (SUB // 8, 8, LANES)

    for outer in range(rows // TABLE):
        cs, ss = cos_s[outer][None], sin_s[outer][None]

        def inner(i, carry, outer=outer, cs=cs, ss=ss):
            off = pl.multiple_of(i * SUB, SUB)
            at = pl.multiple_of(outer * TABLE + i * SUB, SUB)
            x = pad[pl.ds(at + 8, SUB)]
            before = pltpu.roll(jnp.where(lane == LANES - 1, pad[pl.ds(at + 4, SUB)], x), 1, 1)
            after = pltpu.roll(jnp.where(lane == 0, pad[pl.ds(at + 12, SUB)], x), LANES - 1, 1)
            weight = 1.0 / (0.25 * (before + 2.0 * x + after))
            ct = cos_t[pl.ds(off, SUB)].reshape(fold)
            st = sin_t[pl.ds(off, SUB)].reshape(fold)
            cosine = (ct * cs - st * ss).reshape(SUB, LANES)
            sine = (st * cs + ct * ss).reshape(SUB, LANES)
            s_re = strain[0, pl.ds(at, SUB)].astype(jnp.float32)
            s_im = strain[1, pl.ds(at, SUB)].astype(jnp.float32)
            f_re = fid[0, pl.ds(at, SUB)].astype(jnp.float32)
            f_im = fid[1, pl.ds(at, SUB)].astype(jnp.float32)
            cross_re = s_re * f_re + s_im * f_im
            cross_im = s_im * f_re - s_re * f_im
            prod[0, pl.ds(at, SUB)] = (weight * (cross_re * cosine + cross_im * sine)).astype(jnp.bfloat16)
            prod[1, pl.ds(at, SUB)] = (weight * (cross_im * cosine - cross_re * sine)).astype(jnp.bfloat16)
            power[pl.ds(at, SUB)] = (weight * (f_re * f_re + f_im * f_im)).astype(jnp.bfloat16)
            return carry

        lax.fori_loop(0, TABLE // SUB, inner, 0)

    row = lax.broadcasted_iota(jnp.int32, (8, LANES), 0)
    col = lax.broadcasted_iota(jnp.int32, (8, LANES), 1).astype(jnp.float32)
    total = jnp.zeros((8, rows), jnp.float32)
    for q, values in enumerate((prod[0], prod[1], power[...])):
        w = jnp.where(row == 2 * q, 1.0, jnp.where(row == 2 * q + 1, (col + 0.5) / 128.0, 0.0))
        total += lax.dot_general(
            w.astype(jnp.bfloat16), values, (((1,), (1,)), ((), ())),
            preferred_element_type=jnp.float32,
        )
    sums[...] = total


def heterodyne(strain, fid, psd, halo, cos_t, sin_t, cos_s, sin_s):
    total = psd.shape[0]
    rows = min(1024, total)
    steps = total // rows
    per = rows // 8
    return pl.pallas_call(
        het_kernel,
        grid=(steps,),
        in_specs=[
            pl.BlockSpec((2, rows, LANES), lambda i: (0, i, 0)),
            pl.BlockSpec((2, rows, LANES), lambda i: (0, i, 0)),
            pl.BlockSpec((rows, LANES), lambda i: (i, 0)),
            pl.BlockSpec((8, LANES), lambda i: (jnp.maximum(i * per - 1, 0), 0)),
            pl.BlockSpec((8, LANES), lambda i: (jnp.minimum((i + 1) * per, steps * per - 1), 0)),
            pl.BlockSpec((2, 8, LANES), lambda i: (0, 0, 0)),
            pl.BlockSpec((TABLE, LANES), lambda i: (0, 0)),
            pl.BlockSpec((TABLE, LANES), lambda i: (0, 0)),
            pl.BlockSpec((rows // TABLE, 8, LANES), lambda i: (i, 0, 0)),
            pl.BlockSpec((rows // TABLE, 8, LANES), lambda i: (i, 0, 0)),
        ],
        out_specs=[
            pl.BlockSpec((2, rows, LANES), lambda i: (0, i, 0)),
            pl.BlockSpec((8, rows), lambda i: (0, i)),
        ],
        out_shape=[
            jax.ShapeDtypeStruct((2, total, LANES), jnp.bfloat16),
            jax.ShapeDtypeStruct((8, total), jnp.float32),
        ],
        scratch_shapes=[
            pltpu.VMEM((rows + 16, LANES), jnp.float32),
            pltpu.VMEM((rows, LANES), jnp.bfloat16),
        ],
        name="heterodyne",
    )(strain, fid, psd, psd, psd, halo, cos_t, sin_t, cos_s, sin_s)


def pack_kernel(starts, lengths, owners, offsets, prod, packed, sem):
    bins = starts.shape[0]

    def copy(j, c):
        n = lengths[j]
        return pltpu.make_async_copy(
            prod.at[c, pl.ds(starts[j], n)],
            packed.at[owners[j], c, pl.ds(offsets[j], n)],
            sem.at[2 * j + c],
        )

    def start(j, carry):
        copy(j, 0).start()
        copy(j, 1).start()
        return carry

    def wait(j, carry):
        copy(j, 0).wait()
        copy(j, 1).wait()
        return carry

    lax.fori_loop(0, bins, start, 0)
    lax.fori_loop(0, bins, wait, 0)


def pack(starts, lengths, owners, offsets, prod, groups, span):
    return pl.pallas_call(
        pack_kernel,
        grid_spec=pltpu.PrefetchScalarGridSpec(
            num_scalar_prefetch=4,
            in_specs=[pl.BlockSpec(memory_space=pltpu.VMEM)],
            out_specs=pl.BlockSpec(memory_space=pl.ANY),
            scratch_shapes=[pltpu.SemaphoreType.DMA((2 * starts.shape[0],))],
        ),
        out_shape=jax.ShapeDtypeStruct((groups, 2, span) + prod.shape[2:], jnp.bfloat16),
        name="pack",
    )(starts, lengths, owners, offsets, prod)


def unpack_kernel(chunk, pair, lengths, offsets, got, out, work):
    group, m0 = pl.program_id(1), pl.program_id(2) * chunk
    span, rows = got.shape[2], got.shape[3]
    slots = out.shape[2]
    for s in range(slots):
        slot = group * slots + s
        n = lengths[slot] - m0
        base = offsets[slot] + m0

        @pl.when(n > 0)
        def _(s=s, n=n, base=base):
            for m in range(chunk):
                value = got[s // pair, 0, jnp.minimum(base + m, span - 1)].astype(jnp.float32)
                value = jnp.where(m < n, value, 0.0)
                work[m, pl.ds(s, rows, stride=slots)] = value

        @pl.when(n <= 0)
        def _(s=s):
            for m in range(chunk):
                work[m, pl.ds(s, rows, stride=slots)] = jnp.zeros((rows, LANES), jnp.float32)

    for m in range(chunk):
        for r in range(rows):
            out[0, r, :, m * LANES : (m + 1) * LANES] = work[m, r * slots : (r + 1) * slots].astype(jnp.bfloat16)


def unpack(lengths, offsets, got, pair, most):
    groups, _, span, rows, _ = got.shape
    bins = groups * pair
    slots = min(16, bins)
    chunk = min(16, most)
    return pl.pallas_call(
        functools.partial(unpack_kernel, chunk, pair),
        grid_spec=pltpu.PrefetchScalarGridSpec(
            num_scalar_prefetch=2,
            grid=(2, bins // slots, most // chunk),
            in_specs=[
                pl.BlockSpec((slots // pair, 1, span, rows, LANES), lambda c, g, m, *_: (g, c, 0, 0, 0))
            ],
            out_specs=pl.BlockSpec((1, rows, slots, chunk * LANES), lambda c, g, m, *_: (c, 0, g, m)),
            scratch_shapes=[pltpu.VMEM((chunk, rows * slots, LANES), jnp.float32)],
        ),
        out_shape=jax.ShapeDtypeStruct((2, rows, bins, most * LANES), jnp.bfloat16),
        name="unpack",
    )(lengths, offsets, got)


def local(strain, fiducial, psd, time_shift, phase_shift, bin_blocks, bin_owner):
    n_freq = lax.axis_size("freq")
    me = lax.axis_index("freq")
    rows, width = psd.shape
    blocks = width // LANES
    bins = bin_blocks.shape[1]
    pair = bins // n_freq
    most = 2 * blocks // bins
    span = 2 * most

    strain_v = strain.reshape(2, rows, blocks, LANES).transpose(0, 2, 1, 3).reshape(2, blocks * rows, LANES)
    fid_v = fiducial.reshape(2, rows, blocks, LANES).transpose(0, 2, 1, 3).reshape(2, blocks * rows, LANES)
    psd_v = psd.reshape(rows, blocks, LANES).transpose(1, 0, 2).reshape(blocks * rows, LANES)

    up = [(i, i + 1) for i in range(n_freq - 1)]
    down = [(i + 1, i) for i in range(n_freq - 1)]
    halo = jnp.stack([lax.ppermute(psd_v[-8:], "freq", up), lax.ppermute(psd_v[:8], "freq", down)])

    rate = two_pi * time_shift
    total = width * n_freq
    table_blocks = TABLE // rows
    inside = jnp.arange(table_blocks * LANES, dtype=jnp.int32).astype(jnp.float32).reshape(table_blocks, 1, LANES) / total
    inside = (rate[None, :, None] * inside).reshape(TABLE, LANES)
    first = me * width + jnp.arange(blocks // table_blocks, dtype=jnp.int32) * (table_blocks * LANES)
    outer = rate[None, :] * (first.astype(jnp.float32) / total)[:, None] + phase_shift[None, :]
    spread = lambda v: jnp.broadcast_to(jnp.tile(v, (1, 8 // rows))[:, :, None], (v.shape[0], 8, LANES))
    prod, sums = heterodyne(
        strain_v, fid_v, psd_v, halo,
        jnp.cos(inside), jnp.sin(inside), spread(jnp.cos(outer)), spread(jnp.sin(outer)),
    )

    position = jnp.arange(bins, dtype=jnp.int32)
    earlier = (position[None, :] < position[:, None])[None]
    same = bin_owner[:, :, None] == bin_owner[:, None, :]
    both = jnp.logical_and(same, earlier)
    starts = jnp.sum(jnp.where(earlier, bin_blocks[:, None, :], 0), axis=2)
    ranks = jnp.sum(both.astype(jnp.int32), axis=2)
    offsets = jnp.sum(jnp.where(both, bin_blocks[:, None, :], 0), axis=2)
    at_me = lambda a: lax.dynamic_index_in_dim(a, me, 0, keepdims=False)
    my_start, my_len, my_owner, my_off, my_rank = map(at_me, (starts, bin_blocks, bin_owner, offsets, ranks))
    packed = pack(my_start, my_len, my_owner, my_off, prod.reshape(2, blocks, rows, LANES), n_freq, span)

    got = lax.all_to_all(packed, "freq", split_axis=0, concat_axis=0, tiled=True)

    to_me = jnp.logical_and(
        (bin_owner == me)[:, None, :], ranks[:, None, :] == jnp.arange(pair, dtype=jnp.int32)[None, :, None]
    )
    in_len = jnp.sum(jnp.where(to_me, bin_blocks[:, None, :], 0), axis=2).reshape(-1)
    in_off = jnp.sum(jnp.where(to_me, offsets[:, None, :], 0), axis=2).reshape(-1)
    moved = unpack(in_len, in_off, got, pair, most)

    my_slot = my_owner * pair + my_rank
    hot = my_slot[None, :] == position[:, None]
    slot_first = jnp.sum(jnp.where(hot, my_start[None, :], 0), axis=1)
    slot_len = jnp.sum(jnp.where(hot, my_len[None, :], 0), axis=1)
    ids = jnp.arange(blocks, dtype=jnp.int32)
    rel = ids[None, :] - slot_first[:, None]
    live = jnp.logical_and(rel >= 0, rel < slot_len[:, None])
    centre = rel.astype(jnp.float32) - 0.5 * slot_len.astype(jnp.float32)[:, None]
    mask = jnp.where(live, 1.0, 0.0)
    tilt = jnp.where(live, centre, 0.0)
    parts = sums[:6].reshape(3, 2, blocks, rows)
    dot = functools.partial(jnp.einsum, precision=lax.Precision.HIGHEST)
    plain = dot("qbr,sb->qrs", parts[:, 0], mask)
    slope = dot("qbr,sb->qrs", parts[:, 1], mask) + dot("qbr,sb->qrs", parts[:, 0], tilt)
    local_summary = jnp.concatenate(
        [plain[:2] * ratio_scale, slope[:2] * ratio_scale, plain[2:] * power_scale, slope[2:] * power_scale]
    )
    summary = lax.all_to_all(local_summary, "freq", split_axis=2, concat_axis=2, tiled=True)
    return (moved, summary)


def solution(mesh):
    return jax.shard_map(
        local,
        mesh=mesh,
        in_specs=(
            P(None, "tmpl", "freq"),
            P(None, "tmpl", "freq"),
            P("tmpl", "freq"),
            P("tmpl"),
            P("tmpl"),
            P(),
            P(),
        ),
        out_specs=(P(None, "tmpl", "freq", None), P(None, "tmpl", "freq")),
        check_vma=False,
    )
```

time: 435 us -> 212 us (0.49)
  local copies, waits for them, and re-layouts: 210 us -> 16.2 us
  other arithmetic: 131 us -> 6.15 us
  Pallas kernels: 0 us -> 59.9 us
  matrix products: 0 us -> 19.2 us
  waiting for transfers between devices: 72.6 us -> 91.3 us
    gather x9 -> x0, local copies, waits for them, and re-layouts: 125 us -> none  [the longest x3 51.9 us: unpack_blocks(): picked = jnp.take(tiled, block_ids.reshape(-1), axis=1)]
    another operation x5 -> x1, other arithmetic: 87.2 us -> 0.6 us  [local(): jnp.stack([lax.ppermute(psd_v[-8:], 'freq', up), lax.ppermute(psd_v[:8],...]
    pallas_call x0 -> x3, Pallas kernels: none -> 59.9 us  [the longest x1 27.8 us: heterodyne(): pl.pallas_call(het_kernel, grid=(steps,), in_specs=[pl.BlockSpec((2, rows...]
    select_n x7 -> x0, other arithmetic: 25.9 us -> none  [the longest x1 12.5 us: arrange(): picked = jnp.where(live, picked, jnp.zeros((), values.dtype))]
    dot_general x0 -> x3, matrix products: none -> 19.2 us  [the longest x1 7.06 us: local(): dot('qbr,sb->qrs', parts[:, 1], mask)]
    convert_element_type x2 -> x0, local copies, waits for them, and re-layouts: 18.6 us -> none  [heterodyne(): return jnp.stack([prod_re, prod_im, power]).astype(jnp.bfloat16)]
    all_to_all x1, waiting for transfers between devices: 72.6 us -> 89.8 us  [local(): lax.all_to_all(packed, 'freq', split_axis=0, concat_axis=0, tiled=True)]
    scatter x3 -> x0, local copies, waits for them, and re-layouts: 16.3 us -> none  [the longest x1 14.9 us: local(): all_lengths = jnp.zeros((n_freq, n_freq, pair_bins), jnp.int32).at[source...]
  transfers between devices with their start and end apart: 4 -> 4, of which waited for: 1 -> 2; matrix products, arithmetic and copies ran while one was open for 20% -> 4% of each run, Pallas kernels for 0% -> 3%
where the time goes in v1:
time: 212 us; the launch traced here: 211 us
  waiting for transfers between devices  91.3 us (43%)
  Pallas kernels  59.9 us (28%)
  matrix products  19.2 us (9%)
  starting transfers between devices  17.7 us (8%)
  local copies, waits for them, and re-layouts  16.2 us (8%)
  other arithmetic  6.15 us (3%)
    all_to_all x1, waiting for transfers between devices, local(): lax.all_to_all(packed, 'freq', split_axis=0, concat_axis=0, tiled=True)  89.8 us
    pallas_call x1, Pallas kernels, heterodyne(): pl.pallas_call(het_kernel, grid=(steps,), in_specs=[pl.BlockSpec((2, rows...  27.8 us
    pallas_call x1, Pallas kernels, unpack(): pl.pallas_call(functools.partial(unpack_kernel, chunk, pair), grid_spec=p...  26.7 us
    reshape x1, local copies, waits for them, and re-layouts, local(): parts = sums[:6].reshape(3, 2, blocks, rows)  10.3 us
    dot_general x1, matrix products, local(): dot('qbr,sb->qrs', parts[:, 1], mask)  7.06 us
    all_to_all x1, starting transfers between devices, local(): lax.all_to_all(local_summary, 'freq', split_axis=2, concat_axis=2, tiled=...  6.96 us
    dot_general x1, matrix products, local(): dot('qbr,sb->qrs', parts[:, 0], tilt)  6.93 us
    pallas_call x1, Pallas kernels, pack(): pl.pallas_call(pack_kernel, grid_spec=pltpu.PrefetchScalarGridSpec(num_sc...  5.43 us
  transfers between devices with their start and end apart: 4, of which 2 were waited for; matrix products, arithmetic and copies ran while one was open for 4% of the time, Pallas kernels for 3%

profile of v1, /device:TPU:0, one launch (start us, length us, event | category | flops | bytes accessed | tf_op | source)
XLA Modules:
  0.0 211.2 jit_solution(16116758084082432024)
XLA Ops:
  0.6 0.7 fusion.42
  1.3 4.9 %collective-permute-start = (f32[8,128]{1,0:T(8,128)S(1)}, f32[8,128]{1,0:T(8,128)S(1)}, u32[]{:S(2)}, u32[]{:S(2)}) collective-permute-start(f32[8,128]{1,0:T(8,128)S(1)} %bitcast.67), channel_id=1, source_target_pairs={{0,4},{4,8},{8,12},{12,16},{16,20},{20,24},{24,28},{1,5},{5,9},{9,... | collective-permute-start | bytes 12296 | tf_op jit(solution)/shard_map/ppermute | solution.py:205
  6.2 1.3 collective-permute-start.1
  7.6 0.7 broadcast_multiply_fusion
  8.2 0.1 mul.88
  8.3 1.3 select_reduce_fusion
  9.6 1.2 fusion.35
  10.8 0.6 fusion.31
  11.4 0.8 fusion.26
  12.2 1.2 multiply_sine_fusion
  13.5 0.1 select_reduce_fusion.3
  13.8 0.6 pad_maximum_fusion.1.halo
  14.4 0.8 broadcast_in_dim.111.cos_s
  15.1 0.8 broadcast_in_dim.112.sin_s
  15.9 27.8 %heterodyne.1 = (bf16[2,8192,128]{2,1,0:T(8,128)(2,1)}, f32[8,8192]{1,0:T(8,128)}) custom-call(bf16[2,8192,128]{2,1,0:T(8,128)(2,1)} %bitcast.58, bf16[2,8192,128]{2,1,0:T(8,128)(2,1)} %bitcast.59, f32[8192,128]{1,0:T(8,128)} %bitcast.55, f32[8192,128]{1,0:T(8,128)} %bitcast.56, f32[8192,128]{1,0:T(8,128)} %bitcast.57, f32[2,8,128]{2,1,0:T(8,128)} %pad_maximum_fusion.1.halo, ...), custom_call_target="tpu_custom_call" | custom-call | tf_op jit(solution)/shard_map/heterodyne/pallas_call | solution.py:72
  43.7 10.3 %reshape.182 = f32[3,2,2048,4]{3,2,1,0:T(8,128)} reshape(f32[6,8192]{1,0:T(8,128)} %bitcast.62) | data formatting | bytes 393216 | tf_op jit(solution)/shard_map/reshape | solution.py:250
  53.9 7.1 %fusion = f32[3,4,32]{2,1,0:T(4,128)S(1)} fusion(f32[3,2,2048,4]{3,2,1,0:T(8,128)} %reshape.182, s32[32]{0:T(128)S(1)} %get-tuple-element.18, s32[32]{0:T(128)S(1)} %get-tuple-element.17), kind=kOutput, calls=%fused_computation.1 | convolution fusion | flops 9764864 | bytes 3147520 | tf_op jit(solution)/shard_map/qbr,sb->qrs/dot_general | solution.py:253
  61.0 6.9 %fusion.3 = f32[3,4,32]{2,1,0:T(4,128)S(1)} fusion(f32[3,4,32]{2,1,0:T(4,128)S(1)} %fusion, f32[3,2,2048,4]{3,2,1,0:T(8,128)} %reshape.182, f32[32]{0:T(128)S(1)} %convert_multiply_fusion.1, s32[32]{0:T(128)S(1)} %get-tuple-element.17, s32[32]{0:T(128)S(1)} %get-tuple-element.18), kind=kOutput, calls=%fused_computation.5 | convolution fusion | flops 9896320 | bytes 3149184 | tf_op jit(solution)/shard_map/qbr,sb->qrs/dot_general | solution.py:253
  67.9 5.2 %fusion.2 = f32[3,4,32]{2,1,0:T(4,128)S(1)} fusion(f32[3,2,2048,4]{3,2,1,0:T(8,128)S(1)} %copy-done, s32[32]{0:T(128)S(1)} %get-tuple-element.18, s32[32]{0:T(128)S(1)} %get-tuple-element.17), kind=kOutput, calls=%fused_computation.4 | convolution fusion | flops 9764864 | bytes 3148288 | tf_op jit(solution)/shard_map/qbr,sb->qrs/dot_general | solution.py:252
  73.2 0.7 copy.48
  73.9 7.0 %all-to-all-start.1 = ((f32[6,4,32]{0,1,2:T(4,128)}), f32[6,4,32]{0,1,2:T(4,128)S(1)}, u32[]{:S(2)}, u32[]{:S(2)}) async-start(f32[6,4,32]{0,1,2:T(4,128)} %copy.48), calls=%async_computation.1 | async-start | bytes 131072 | tf_op jit(solution)/shard_map/all_to_all | solution.py:257
  80.9 5.4 %pack.1 = bf16[8,2,256,4,128]{4,3,2,1,0:T(4,128)(2,1)} custom-call(s32[32]{0:T(128)} %copy-done.4, s32[32]{0:T(128)} %copy-done.3, s32[32]{0:T(128)} %get-tuple-element.24.owners, s32[32]{0:T(128)} %get-tuple-element.28.offsets, bf16[2,2048,4,128]{3,2,1,0:T(4,128)(2,1)} %bitcast.60), custom_call_target="tpu_custom_call" | custom-call | tf_op jit(solution)/shard_map/pack/pallas_call | solution.py:129
  86.3 1.4 all-to-all-done.1
  87.8 4.6 %all-to-all-start = ((bf16[8,2,256,4,128]{4,3,2,1,0:T(4,128)(2,1)}), bf16[8,2,256,4,128]{4,3,2,1,0:T(4,128)(2,1)}, u32[]{:S(2)}, u32[]{:S(2)}) async-start(bf16[8,2,256,4,128]{4,3,2,1,0:T(4,128)(2,1)} %pack.1), calls=%async_computation | async-start | bytes 8388608 | tf_op jit(solution)/shard_map/all_to_all | solution.py:231
  92.4 0.2 select_reduce_fusion.4
  92.6 0.1 copy.39
  92.7 0.6 reshape.173.lengths
  93.3 0.1 copy.40
  93.4 0.6 reshape.174.offsets
  94.0 0.7 copy.49
  94.7 89.8 %all-to-all-done.got = bf16[8,2,256,4,128]{4,3,2,1,0:T(4,128)(2,1)} async-done(((bf16[8,2,256,4,128]{4,3,2,1,0:T(4,128)(2,1)}), bf16[8,2,256,4,128]{4,3,2,1,0:T(4,128)(2,1)}, u32[]{:S(2)}, u32[]{:S(2)}) %all-to-all-start) | async-done | bytes 4194336 | tf_op jit(solution)/shard_map/all_to_all | solution.py:231
  184.6 26.7 %unpack.1 = bf16[2,4,32,16384]{3,2,1,0:T(8,128)(2,1)} custom-call(s32[32]{0:T(128)} %reshape.173.lengths, s32[32]{0:T(128)} %reshape.174.offsets, bf16[8,2,256,4,128]{4,3,2,1,0:T(4,128)(2,1)} %all-to-all-done.got), custom_call_target="tpu_custom_call" | custom-call | tf_op jit(solution)/shard_map/unpack/pallas_call | solution.py:173
  (28 shorter events, 0.3 us)
Async XLA Ops:
  1.3 12.4 %collective-permute-start = (f32[8,128]{1,0:T(8,128)S(1)}, f32[8,128]{1,0:T(8,128)S(1)}, u32[]{:S(2)}, u32[]{:S(2)}) collective-permute-start(f32[8,128]{1,0:T(8,128)S(1)} %bitcast.67), channel_id=1, source_target_pairs={{0,4},{4,8},{8,12},{12,16},{16,20},{20,24},{24,28},{1,5},{5,9},{9,... | collective-permute-start | bytes 12296 | tf_op jit(solution)/shard_map/ppermute | solution.py:205
  6.2 7.5 %collective-permute-start.1 = (f32[8,128]{1,0:T(8,128)S(1)}, f32[8,128]{1,0:T(8,128)S(1)}, u32[]{:S(2)}, u32[]{:S(2)}) collective-permute-start(f32[8,128]{1,0:T(8,128)S(1)} %bitcast.66), channel_id=1, source_target_pairs={{4,0},{8,4},{12,8},{16,12},{20,16},{24,20},{28,24},{5,1},{9,5},{13... | collective-permute-start | bytes 12296 | tf_op jit(solution)/shard_map/ppermute | solution.py:205
  10.8 32.8 %copy-start.3 = (s32[32]{0:T(128)}, s32[32]{0:T(128)S(1)}, u32[]{:S(2)}) copy-start(s32[32]{0:T(128)S(1)} %get-tuple-element.29.lengths) | copy-start | bytes 388
  11.4 32.2 %copy-start.4 = (s32[32]{0:T(128)}, s32[32]{0:T(128)S(1)}, u32[]{:S(2)}) copy-start(s32[32]{0:T(128)S(1)} %get-tuple-element.27.starts) | copy-start | bytes 388
  53.9 14.0 %copy-start = (f32[3,2,2048,4]{3,2,1,0:T(8,128)S(1)}, f32[3,2,2048,4]{3,2,1,0:T(8,128)}, u32[]{:S(2)}) copy-start(f32[3,2,2048,4]{3,2,1,0:T(8,128)} %reshape.182) | copy-start | bytes 589828
  73.9 13.9 %all-to-all-start.1 = ((f32[6,4,32]{0,1,2:T(4,128)}), f32[6,4,32]{0,1,2:T(4,128)S(1)}, u32[]{:S(2)}, u32[]{:S(2)}) async-start(f32[6,4,32]{0,1,2:T(4,128)} %copy.48), calls=%async_computation.1 | async-start | bytes 131072 | tf_op jit(solution)/shard_map/all_to_all | solution.py:257
  86.3 6.1 %copy-start.1 = (s32[8,32]{1,0:T(8,128)S(1)}, s32[8,32]{1,0:T(8,128)}, u32[]{:S(2)}) copy-start(s32[8,32]{1,0:T(8,128)} %param.13) | copy-start | bytes 3076
  86.3 6.1 %copy-start.2 = (s32[8,32]{1,0:T(8,128)S(1)}, s32[8,32]{1,0:T(8,128)}, u32[]{:S(2)}) copy-start(s32[8,32]{1,0:T(8,128)} %param.12) | copy-start | bytes 3076
  87.8 96.8 %all-to-all-start = ((bf16[8,2,256,4,128]{4,3,2,1,0:T(4,128)(2,1)}), bf16[8,2,256,4,128]{4,3,2,1,0:T(4,128)(2,1)}, u32[]{:S(2)}, u32[]{:S(2)}) async-start(bf16[8,2,256,4,128]{4,3,2,1,0:T(4,128)(2,1)} %pack.1), calls=%async_computation | async-start | bytes 8388608 | tf_op jit(solution)/shard_map/all_to_all | solution.py:231

commit v2 on v1

v2 whole, which is shorter than its diff:
```python
import functools
import math

import jax
import jax.numpy as jnp
from jax import lax
from jax.experimental import pallas as pl
from jax.experimental.pallas import tpu as pltpu
from jax.sharding import PartitionSpec as P


two_pi = 2.0 * math.pi
ratio_scale = 1.0 / 64.0
power_scale = 1.0 / 2048.0
LANES = 128
SUB = 32
TABLE = 256


def het_kernel(strain, fid, psd, prev, nxt, halo, cos_t, sin_t, cos_s, sin_s, real, imag, power, pad):
    rows = psd.shape[0]
    step, last = pl.program_id(0), pl.num_programs(0) - 1
    pad[8 : 8 + rows] = psd[...]
    pad[0:8] = jnp.where(step == 0, halo[0], prev[...])
    pad[8 + rows : 16 + rows] = jnp.where(step == last, halo[1], nxt[...])
    lane = lax.broadcasted_iota(jnp.int32, (SUB, LANES), 1)
    fold = (SUB // 8, 8, LANES)

    for outer in range(rows // TABLE):
        cs, ss = cos_s[outer][None], sin_s[outer][None]

        def inner(i, carry, outer=outer, cs=cs, ss=ss):
            off = pl.multiple_of(i * SUB, SUB)
            at = pl.multiple_of(outer * TABLE + i * SUB, SUB)
            x = pad[pl.ds(at + 8, SUB)]
            before = pltpu.roll(jnp.where(lane == LANES - 1, pad[pl.ds(at + 4, SUB)], x), 1, 1)
            after = pltpu.roll(jnp.where(lane == 0, pad[pl.ds(at + 12, SUB)], x), LANES - 1, 1)
            weight = 1.0 / (0.25 * (before + 2.0 * x + after))
            ct = cos_t[pl.ds(off, SUB)].reshape(fold)
            st = sin_t[pl.ds(off, SUB)].reshape(fold)
            cosine = (ct * cs - st * ss).reshape(SUB, LANES)
            sine = (st * cs + ct * ss).reshape(SUB, LANES)
            s_re = strain[0, pl.ds(at, SUB)].astype(jnp.float32)
            s_im = strain[1, pl.ds(at, SUB)].astype(jnp.float32)
            f_re = fid[0, pl.ds(at, SUB)].astype(jnp.float32)
            f_im = fid[1, pl.ds(at, SUB)].astype(jnp.float32)
            cross_re = s_re * f_re + s_im * f_im
            cross_im = s_im * f_re - s_re * f_im
            real[pl.ds(at, SUB)] = (weight * (cross_re * cosine + cross_im * sine)).astype(jnp.bfloat16)
            imag[pl.ds(at, SUB)] = (weight * (cross_im * cosine - cross_re * sine)).astype(jnp.bfloat16)
            power[pl.ds(at, SUB)] = (weight * (f_re * f_re + f_im * f_im)).astype(jnp.bfloat16)
            return carry

        lax.fori_loop(0, TABLE // SUB, inner, 0)


def heterodyne(strain, fid, psd, halo, cos_t, sin_t, cos_s, sin_s):
    total = psd.shape[0]
    rows = min(1024, total)
    steps = total // rows
    per = rows // 8
    return pl.pallas_call(
        het_kernel,
        grid=(steps,),
        in_specs=[
            pl.BlockSpec((2, rows, LANES), lambda i: (0, i, 0)),
            pl.BlockSpec((2, rows, LANES), lambda i: (0, i, 0)),
            pl.BlockSpec((rows, LANES), lambda i: (i, 0)),
            pl.BlockSpec((8, LANES), lambda i: (jnp.maximum(i * per - 1, 0), 0)),
            pl.BlockSpec((8, LANES), lambda i: (jnp.minimum((i + 1) * per, steps * per - 1), 0)),
            pl.BlockSpec((2, 8, LANES), lambda i: (0, 0, 0)),
            pl.BlockSpec((TABLE, LANES), lambda i: (0, 0)),
            pl.BlockSpec((TABLE, LANES), lambda i: (0, 0)),
            pl.BlockSpec((rows // TABLE, 8, LANES), lambda i: (i, 0, 0)),
            pl.BlockSpec((rows // TABLE, 8, LANES), lambda i: (i, 0, 0)),
        ],
        out_specs=[pl.BlockSpec((rows, LANES), lambda i: (i, 0))] * 3,
        out_shape=[jax.ShapeDtypeStruct((total, LANES), jnp.bfloat16)] * 3,
        scratch_shapes=[pltpu.VMEM((rows + 16, LANES), jnp.float32)],
        cost_estimate=pl.CostEstimate(flops=60 * total * LANES, bytes_accessed=18 * total * LANES, transcendentals=0),
        name="heterodyne",
    )(strain, fid, psd, psd, psd, halo, cos_t, sin_t, cos_s, sin_s)


def sums_kernel(tmpl_rows, real, imag, power, first, length, flat, tilted):
    rows = real.shape[0]
    cols = flat.shape[1]
    step = pl.program_id(0)
    row = lax.broadcasted_iota(jnp.int32, (8, LANES), 0)
    col = lax.broadcasted_iota(jnp.int32, (8, LANES), 1).astype(jnp.float32)
    lanes = jnp.zeros((8, rows), jnp.float32)
    for q, values in enumerate((real, imag, power)):
        w = jnp.where(row == 2 * q, 1.0, jnp.where(row == 2 * q + 1, (col + 0.5) / 128.0, 0.0))
        lanes += lax.dot_general(
            w.astype(jnp.bfloat16), values[...], (((1,), (1,)), ((), ())),
            preferred_element_type=jnp.float32,
        )
    index = lax.broadcasted_iota(jnp.int32, (rows, cols), 0)
    slot_row = lax.broadcasted_iota(jnp.int32, (rows, cols), 1) // (cols // tmpl_rows)
    rel = step * (rows // tmpl_rows) + index // tmpl_rows - first[...]
    live = (index % tmpl_rows == slot_row) & (rel >= 0) & (rel < length[...])
    mask = jnp.where(live, 1.0, 0.0)
    tilt = jnp.where(live, rel.astype(jnp.float32) - 0.5 * length[...].astype(jnp.float32), 0.0)

    @pl.when(step == 0)
    def _():
        flat[...] = jnp.zeros_like(flat)
        tilted[...] = jnp.zeros_like(tilted)

    dot = functools.partial(jnp.dot, precision=lax.Precision.HIGHEST, preferred_element_type=jnp.float32)
    flat[...] += dot(lanes, mask)
    tilted[...] += dot(lanes, tilt)


def bin_sums(tmpl_rows, real, imag, power, first, length):
    total = real.shape[0]
    rows = min(1024, total)
    cols = first.shape[1]
    block = pl.BlockSpec((rows, LANES), lambda i: (i, 0))
    table = pl.BlockSpec((1, cols), lambda i: (0, 0))
    return pl.pallas_call(
        functools.partial(sums_kernel, tmpl_rows),
        grid=(total // rows,),
        in_specs=[block, block, block, table, table],
        out_specs=[pl.BlockSpec((8, cols), lambda i: (0, 0))] * 2,
        out_shape=[jax.ShapeDtypeStruct((8, cols), jnp.float32)] * 2,
        cost_estimate=pl.CostEstimate(flops=200 * total * LANES, bytes_accessed=6 * total * LANES, transcendentals=0),
        name="sums",
    )(real, imag, power, first, length)


def pack_kernel(starts, lengths, offsets, prod, *rest):
    *packed, sem = rest
    pair = starts.shape[0] // len(packed)

    def copies():
        for step, target in enumerate(packed):
            for rank in range(pair):
                j = step * pair + rank
                n = lengths[j]
                yield pltpu.make_async_copy(
                    prod.at[pl.ds(starts[j], n)], target.at[pl.ds(offsets[j], n)], sem.at[j]
                )

    for copy in copies():
        copy.start()
    for copy in copies():
        copy.wait()


def pack(starts, lengths, offsets, prod, groups, span):
    shape = jax.ShapeDtypeStruct((span,) + prod.shape[1:], jnp.bfloat16)
    return pl.pallas_call(
        pack_kernel,
        grid_spec=pltpu.PrefetchScalarGridSpec(
            num_scalar_prefetch=3,
            in_specs=[pl.BlockSpec(memory_space=pltpu.VMEM)],
            out_specs=[pl.BlockSpec(memory_space=pl.ANY)] * groups,
            scratch_shapes=[pltpu.SemaphoreType.DMA((starts.shape[0],))],
        ),
        out_shape=[shape] * groups,
        cost_estimate=pl.CostEstimate(flops=0, bytes_accessed=4 * prod.size, transcendentals=0),
        name="pack",
    )(starts, lengths, offsets, prod)


def unpack_kernel(chunk, pair, unit, where, lengths, offsets, near, far, *rest):
    out, work = rest[-2:]
    m0 = pl.program_id(0) * chunk
    span, rows = near.shape[0], near.shape[1]
    slots = out.shape[2]
    for half, got in enumerate((near, far)):
        base_slot = (where[1] ^ half) * pair
        for rank in range(pair):
            j = (2 * unit + half) * pair + rank
            n = lengths[j] - m0
            base = offsets[j] + m0
            lane = base_slot + rank

            @pl.when(n > 0)
            def _(got=got, n=n, base=base, lane=lane):
                for m in range(chunk):
                    value = got[jnp.minimum(base + m, span - 1)].astype(jnp.float32)
                    value = jnp.where(m < n, value, 0.0)
                    work[m, pl.ds(lane, rows, stride=slots)] = value

            @pl.when(n <= 0)
            def _(lane=lane):
                for m in range(chunk):
                    work[m, pl.ds(lane, rows, stride=slots)] = jnp.zeros((rows, LANES), jnp.float32)

    for m in range(chunk):
        for r in range(rows):
            out[0, r, :, m * LANES : (m + 1) * LANES] = work[m, r * slots : (r + 1) * slots].astype(jnp.bfloat16)


def unpack(part, unit, where, lengths, offsets, near, far, dest, bins, pair, most):
    span, rows, _ = near.shape
    slots = 2 * pair
    chunk = min(16, most)
    whole = pl.BlockSpec((span, rows, LANES), lambda m, *_: (0, 0, 0))
    extra = [] if dest is None else [dest]
    size = rows * slots * most * LANES
    return pl.pallas_call(
        functools.partial(unpack_kernel, chunk, pair, unit),
        grid_spec=pltpu.PrefetchScalarGridSpec(
            num_scalar_prefetch=3,
            grid=(most // chunk,),
            in_specs=[whole, whole] + [pl.BlockSpec(memory_space=pl.ANY)] * len(extra),
            out_specs=pl.BlockSpec(
                (1, rows, slots, chunk * LANES), lambda m, w, *_: (part, 0, w[0] ^ unit, m)
            ),
            scratch_shapes=[pltpu.VMEM((chunk, rows * slots, LANES), jnp.float32)],
        ),
        out_shape=jax.ShapeDtypeStruct((2, rows, bins, most * LANES), jnp.bfloat16),
        input_output_aliases={5: 0} if extra else {},
        cost_estimate=pl.CostEstimate(flops=8 * size, bytes_accessed=3 * size, transcendentals=0),
        name="unpack",
    )(where, lengths, offsets, near, far, *extra)


def local(strain, fiducial, psd, time_shift, phase_shift, bin_blocks, bin_owner):
    n_freq = lax.axis_size("freq")
    me = lax.axis_index("freq")
    rows, width = psd.shape
    blocks = width // LANES
    bins = bin_blocks.shape[1]
    pair = bins // n_freq
    most = 2 * blocks // bins
    span = 2 * most

    strain_v = strain.reshape(2, rows, blocks, LANES).transpose(0, 2, 1, 3).reshape(2, blocks * rows, LANES)
    fid_v = fiducial.reshape(2, rows, blocks, LANES).transpose(0, 2, 1, 3).reshape(2, blocks * rows, LANES)
    psd_v = psd.reshape(rows, blocks, LANES).transpose(1, 0, 2).reshape(blocks * rows, LANES)

    up = [(i, i + 1) for i in range(n_freq - 1)]
    down = [(i + 1, i) for i in range(n_freq - 1)]
    halo = jnp.stack([lax.ppermute(psd_v[-8:], "freq", up), lax.ppermute(psd_v[:8], "freq", down)])

    rate = two_pi * time_shift
    total = width * n_freq
    table_blocks = TABLE // rows
    inside = jnp.arange(table_blocks * LANES, dtype=jnp.int32).astype(jnp.float32).reshape(table_blocks, 1, LANES) / total
    inside = (rate[None, :, None] * inside).reshape(TABLE, LANES)
    first = me * width + jnp.arange(blocks // table_blocks, dtype=jnp.int32) * (table_blocks * LANES)
    outer = rate[None, :] * (first.astype(jnp.float32) / total)[:, None] + phase_shift[None, :]
    spread = lambda v: jnp.broadcast_to(jnp.tile(v, (1, 8 // rows))[:, :, None], (v.shape[0], 8, LANES))
    real, imag, power = heterodyne(
        strain_v, fid_v, psd_v, halo,
        jnp.cos(inside), jnp.sin(inside), spread(jnp.cos(outer)), spread(jnp.sin(outer)),
    )

    position = jnp.arange(bins, dtype=jnp.int32)
    earlier = (position[None, :] < position[:, None])[None]
    same = bin_owner[:, :, None] == bin_owner[:, None, :]
    both = jnp.logical_and(same, earlier)
    starts = jnp.sum(jnp.where(earlier, bin_blocks[:, None, :], 0), axis=2)
    ranks = jnp.sum(both.astype(jnp.int32), axis=2)
    offsets = jnp.sum(jnp.where(both, bin_blocks[:, None, :], 0), axis=2)
    at_me = lambda a: lax.dynamic_index_in_dim(a, me, 0, keepdims=False)
    my_start, my_len, my_owner, my_off, my_rank = map(at_me, (starts, bin_blocks, bin_owner, offsets, ranks))

    pick = lambda key, values: jnp.sum(
        jnp.where(key[None, :] == position[:, None], values[None, :], 0), axis=1
    )
    by_step = (my_owner ^ me) * pair + my_rank
    send_start, send_len, send_off = (pick(by_step, v) for v in (my_start, my_len, my_off))
    peers = jnp.arange(n_freq, dtype=jnp.int32) ^ me
    to_me = jnp.logical_and(
        (bin_owner == me)[:, None, :], ranks[:, None, :] == jnp.arange(pair, dtype=jnp.int32)[None, :, None]
    )
    to_me = jnp.logical_and(to_me[None], (peers[:, None] == jnp.arange(n_freq)[None, :])[:, :, None, None])
    in_len = jnp.sum(jnp.where(to_me, bin_blocks[None, :, None, :], 0), axis=(1, 3)).reshape(-1)
    in_off = jnp.sum(jnp.where(to_me, offsets[None, :, None, :], 0), axis=(1, 3)).reshape(-1)
    where = jnp.stack([me // 2, me % 2]).astype(jnp.int32)

    steps = list(range(n_freq // 2, n_freq)) + list(range(1, n_freq // 2))
    got = []
    for values in (real, imag):
        packed = pack(send_start, send_len, send_off, values.reshape(blocks, rows, LANES), n_freq, span)
        here = {0: packed[0]}
        for s in steps:
            here[s] = lax.ppermute(packed[s], "freq", [(i, i ^ s) for i in range(n_freq)])
        got.append(here)

    my_slot = my_owner * pair + my_rank
    slot_first, slot_len = pick(my_slot, my_start), pick(my_slot, my_len)
    flat, tilted = bin_sums(rows, real, imag, power, jnp.tile(slot_first, rows)[None], jnp.tile(slot_len, rows)[None])
    flat = flat[:6].reshape(3, 2, rows, bins)
    plain = flat[:, 0]
    slope = flat[:, 1] + tilted[:6].reshape(3, 2, rows, bins)[:, 0]
    local_summary = jnp.concatenate(
        [plain[:2] * ratio_scale, slope[:2] * ratio_scale, plain[2:] * power_scale, slope[2:] * power_scale]
    )
    summary = lax.all_to_all(local_summary, "freq", split_axis=2, concat_axis=2, tiled=True)

    moved = None
    half = n_freq // 4
    units = list(range(half)) + list(range(half, 2 * half))
    for part in range(2):
        for unit in units:
            moved = unpack(
                part, unit, where, in_len, in_off, got[part][2 * unit], got[part][2 * unit + 1],
                moved, bins, pair, most,
            )
    return (moved, summary)


def solution(mesh):
    return jax.shard_map(
        local,
        mesh=mesh,
        in_specs=(
            P(None, "tmpl", "freq"),
            P(None, "tmpl", "freq"),
            P("tmpl", "freq"),
            P("tmpl"),
            P("tmpl"),
            P(),
            P(),
        ),
        out_specs=(P(None, "tmpl", "freq", None), P(None, "tmpl", "freq")),
        check_vma=False,
    )
```

time: 212 us -> 216 us (1.019)
  waiting for transfers between devices: 91.3 us -> 44.3 us
  starting transfers between devices: 17.7 us -> 59.4 us
  Pallas kernels: 59.9 us -> 90.6 us
  matrix products: 19.2 us -> 0 us
  local copies, waits for them, and re-layouts: 16.2 us -> 10.8 us
  other arithmetic: 6.15 us -> 9.42 us
    all_to_all x1 -> x0, waiting for transfers between devices: 89.8 us -> none  [local(): lax.all_to_all(packed, 'freq', split_axis=0, concat_axis=0, tiled=True)]
    ppermute x0 -> x14, starting transfers between devices: none -> 45.5 us  [local(): lax.ppermute(packed[s], 'freq', [(i, i ^ s) for i in range(n_freq)])]
    pallas_call x1 -> x9, Pallas kernels: 26.7 us -> 57.2 us  [the longest x8 46.7 us: unpack(): pl.pallas_call(functools.partial(unpack_kernel, chunk, pair, unit), grid_...]
    all_to_all x1, waiting for transfers between devices: 1.44 us -> 26.6 us  [local(): lax.all_to_all(local_summary, 'freq', split_axis=2, concat_axis=2, tiled=...]
    dot_general x3 -> x0, matrix products: 19.2 us -> none  [the longest x1 7.06 us: local(): dot('qbr,sb->qrs', parts[:, 1], mask)]
    ppermute x0 -> x14, waiting for transfers between devices: none -> 17.7 us  [local(): lax.ppermute(packed[s], 'freq', [(i, i ^ s) for i in range(n_freq)])]
    reshape x3 -> x4, local copies, waits for them, and re-layouts: 11.5 us -> 2.72 us  [the longest x1 0.76 us: local(): flat = flat[:6].reshape(3, 2, rows, bins)]
    all_to_all x1 -> x0, starting transfers between devices: 4.6 us -> none  [local(): lax.all_to_all(packed, 'freq', split_axis=0, concat_axis=0, tiled=True)]
  transfers between devices with their start and end apart: 4 -> 17, of which waited for: 2 -> 3; matrix products, arithmetic and copies ran while one was open for 4% -> 6% of each run, Pallas kernels for 3% -> 21%
where the time goes in v2:
time: 216 us; the launch traced here: 215 us
  Pallas kernels  90.6 us (42%)
  starting transfers between devices  59.4 us (28%)
  waiting for transfers between devices  44.3 us (21%)
  local copies, waits for them, and re-layouts  10.8 us (5%)
  other arithmetic  9.42 us (4%)
    pallas_call x8, Pallas kernels, unpack(): pl.pallas_call(functools.partial(unpack_kernel, chunk, pair, unit), grid_...  46.7 us
    ppermute x14, starting transfers between devices, local(): lax.ppermute(packed[s], 'freq', [(i, i ^ s) for i in range(n_freq)])  45.5 us
    all_to_all x1, waiting for transfers between devices, local(): lax.all_to_all(local_summary, 'freq', split_axis=2, concat_axis=2, tiled=...  26.6 us
    pallas_call x1, Pallas kernels, heterodyne(): pl.pallas_call(het_kernel, grid=(steps,), in_specs=[pl.BlockSpec((2, rows...  25.7 us
    ppermute x14, waiting for transfers between devices, local(): lax.ppermute(packed[s], 'freq', [(i, i ^ s) for i in range(n_freq)])  17.7 us
    pallas_call x1, Pallas kernels, bin_sums(): pl.pallas_call(functools.partial(sums_kernel, tmpl_rows), grid=(total //...  10.5 us
    pallas_call x2, Pallas kernels, pack(): pl.pallas_call(pack_kernel, grid_spec=pltpu.PrefetchScalarGridSpec(num_sc...  7.72 us
    all_to_all x1, starting transfers between devices, local(): lax.all_to_all(local_summary, 'freq', split_axis=2, concat_axis=2, tiled=...  7.17 us
  transfers between devices with their start and end apart: 17, of which 3 were waited for; matrix products, arithmetic and copies ran while one was open for 6% of the time, Pallas kernels for 21%

profile of v2, /device:TPU:0, one launch (start us, length us, event | category | flops | bytes accessed | tf_op | source)
XLA Modules:
  0.0 215.4 jit_solution(200349851630925775)
XLA Ops:
  1.3 1.3 collective-permute-start.1
  2.6 5.5 %collective-permute-start = (f32[8,128]{1,0:T(8,128)S(1)}, f32[8,128]{1,0:T(8,128)S(1)}, u32[]{:S(2)}, u32[]{:S(2)}) collective-permute-start(f32[8,128]{1,0:T(8,128)S(1)} %bitcast.78), channel_id=1, source_target_pairs={{0,4},{4,8},{8,12},{12,16},{16,20},{20,24},{24,28},{1,5},{5,9},{9,... | collective-permute-start | bytes 12296 | tf_op jit(solution)/shard_map/ppermute | solution.py:238
  9.6 1.3 select_reduce_fusion
  11.8 0.8 fusion.10
  12.6 2.0 fusion.1
  14.6 1.2 multiply_sine_fusion
  20.1 25.7 %heterodyne.1 = (bf16[8192,128]{1,0:T(8,128)(2,1)}, bf16[8192,128]{1,0:T(8,128)(2,1)}, bf16[8192,128]{1,0:T(8,128)(2,1)}) custom-call(bf16[2,8192,128]{2,1,0:T(8,128)(2,1)} %bitcast.72, bf16[2,8192,128]{2,1,0:T(8,128)(2,1)} %bitcast.73, f32[8192,128]{1,0:T(8,128)} %bitcast.67, f32[8192,128]{1,0:T(8,128)} %bitcast.68, f32[8192,128]{1,0:T(8,128)} %bitcast.69, ...), custom_call_target="tpu_custom_call" | custom-call | flops 62914560 | bytes 18874368 | tf_op jit(solution)/shard_map/heterodyne/pallas_call | solution.py:62
  45.8 10.5 %sums.1 = (f32[8,128]{1,0:T(8,128)}, f32[8,128]{1,0:T(8,128)}) custom-call(bf16[8192,128]{1,0:T(8,128)(2,1)} %get-tuple-element.32.real, bf16[8192,128]{1,0:T(8,128)(2,1)} %get-tuple-element.23.imag, bf16[8192,128]{1,0:T(8,128)(2,1)} %get-tuple-element.41.power, s32[1,128]{1,0:T(1,128)} %broadcast_in_dim_tile.8.first, s32[1,128]{1,0:T(1,128)} %broadcast_in_dim_tile.9.length), custom_call_target="tpu_custom_call" | custom-call | flops 209715200 | bytes 6291456 | tf_op jit(solution)/shard_map/sums/pallas_call | solution.py:121
  57.1 3.9 %pack.3 = (bf16[256,4,128]{2,1,0:T(4,128)(2,1)}, bf16[256,4,128]{2,1,0:T(4,128)(2,1)}, bf16[256,4,128]{2,1,0:T(4,128)(2,1)}, bf16[256,4,128]{2,1,0:T(4,128)(2,1)...) custom-call(s32[32]{0:T(128)} %get-tuple-element.58.starts, ...), custom_call_target="tpu_custom_call" | custom-call | bytes 4194304 | tf_op jit(solution)/shard_map/pack/pallas_call | solution.py:153
  60.9 4.2 %collective-permute-start.9 = (bf16[256,4,128]{2,1,0:T(4,128)(2,1)}, bf16[256,4,128]{2,1,0:T(4,128)(2,1)S(1)}, u32[]{:S(2)}, u32[]{:S(2)}) collective-permute-start(bf16[256,4,128]{2,1,0:T(4,128)(2,1)} %get-tuple-element.33), channel_id=1, source_target_pairs={{0,24},{4,28},{8,16},{12,20},{16,8},{20,12},{24,0},{28,4},{1,25},{... | collective-permute-start | bytes 786440 | tf_op jit(solution)/shard_map/ppermute | solution.py:283
  65.1 2.1 collective-permute-start.10
  67.2 0.8 collective-permute-start.11
  68.0 1.1 collective-permute-start.12
  69.0 3.8 %pack.2 = (bf16[256,4,128]{2,1,0:T(4,128)(2,1)}, bf16[256,4,128]{2,1,0:T(4,128)(2,1)}, bf16[256,4,128]{2,1,0:T(4,128)(2,1)}, bf16[256,4,128]{2,1,0:T(4,128)(2,1)...) custom-call(s32[32]{0:T(128)} %get-tuple-element.58.starts, ...), custom_call_target="tpu_custom_call" | custom-call | bytes 4194304 | tf_op jit(solution)/shard_map/pack/pallas_call | solution.py:153
  73.6 1.4 collective-permute-start.13
  75.0 20.9 %collective-permute-start.14 = (bf16[256,4,128]{2,1,0:T(4,128)(2,1)}, bf16[256,4,128]{2,1,0:T(4,128)(2,1)S(1)}, u32[]{:S(2)}, u32[]{:S(2)}) collective-permute-start(bf16[256,4,128]{2,1,0:T(4,128)(2,1)} %get-tuple-element.38), channel_id=1, source_target_pairs={{0,12},{4,8},{8,4},{12,0},{16,28},{20,24},{24,20},{28,16},{1,13},{... | collective-permute-start | bytes 786440 | tf_op jit(solution)/shard_map/ppermute | solution.py:283
  96.0 9.0 %collective-permute-done.11.near = bf16[256,4,128]{2,1,0:T(4,128)(2,1)S(1)} collective-permute-done((bf16[256,4,128]{2,1,0:T(4,128)(2,1)}, bf16[256,4,128]{2,1,0:T(4,128)(2,1)S(1)}, u32[]{:S(2)}, u32[]{:S(2)}) %collective-permute-start.11) | collective-permute-done | bytes 262176 | tf_op jit(solution)/shard_map/ppermute | solution.py:283
  105.4 8.7 %collective-permute-done.12.far = bf16[256,4,128]{2,1,0:T(4,128)(2,1)S(1)} collective-permute-done((bf16[256,4,128]{2,1,0:T(4,128)(2,1)}, bf16[256,4,128]{2,1,0:T(4,128)(2,1)S(1)}, u32[]{:S(2)}, u32[]{:S(2)}) %collective-permute-start.12) | collective-permute-done | bytes 262176 | tf_op jit(solution)/shard_map/ppermute | solution.py:283
  114.2 2.5 %collective-permute-start.2 = (bf16[256,4,128]{2,1,0:T(4,128)(2,1)}, bf16[256,4,128]{2,1,0:T(4,128)(2,1)S(1)}, u32[]{:S(2)}, u32[]{:S(2)}) collective-permute-start(bf16[256,4,128]{2,1,0:T(4,128)(2,1)} %get-tuple-element.24), channel_id=1, source_target_pairs={{0,24},{4,28},{8,16},{12,20},{16,8},{20,12},{24,0},{28,4},{1,25},{... | collective-permute-start | bytes 786440 | tf_op jit(solution)/shard_map/ppermute | solution.py:283
  116.7 2.9 %collective-permute-start.3 = (bf16[256,4,128]{2,1,0:T(4,128)(2,1)}, bf16[256,4,128]{2,1,0:T(4,128)(2,1)S(1)}, u32[]{:S(2)}, u32[]{:S(2)}) collective-permute-start(bf16[256,4,128]{2,1,0:T(4,128)(2,1)} %get-tuple-element.25), channel_id=1, source_target_pairs={{0,28},{4,24},{8,20},{12,16},{16,12},{20,8},{24,4},{28,0},{1,29},{... | collective-permute-start | bytes 786440 | tf_op jit(solution)/shard_map/ppermute | solution.py:283
  119.6 2.4 %collective-permute-start.5 = (bf16[256,4,128]{2,1,0:T(4,128)(2,1)}, bf16[256,4,128]{2,1,0:T(4,128)(2,1)S(1)}, u32[]{:S(2)}, u32[]{:S(2)}) collective-permute-start(bf16[256,4,128]{2,1,0:T(4,128)(2,1)} %get-tuple-element.27), channel_id=1, source_target_pairs={{0,20},{4,16},{8,28},{12,24},{16,4},{20,0},{24,12},{28,8},{1,21},{... | collective-permute-start | bytes 786440 | tf_op jit(solution)/shard_map/ppermute | solution.py:283
  121.9 6.9 %collective-permute-start.7 = (bf16[256,4,128]{2,1,0:T(4,128)(2,1)}, bf16[256,4,128]{2,1,0:T(4,128)(2,1)}, u32[]{:S(2)}, u32[]{:S(2)}) collective-permute-start(bf16[256,4,128]{2,1,0:T(4,128)(2,1)} %get-tuple-element.29), channel_id=1, source_target_pairs={{0,12},{4,8},{8,4},{12,0},{16,28},{20,24},{24,20},{28,16},{1,13},{... | collective-permute-start | bytes 786440 | tf_op jit(solution)/shard_map/ppermute | solution.py:283
  129.6 7.2 %all-to-all-start = ((f32[6,4,32]{0,1,2:T(4,128)}), f32[6,4,32]{0,1,2:T(4,128)S(1)}, u32[]{:S(2)}, u32[]{:S(2)}) async-start(f32[6,4,32]{0,1,2:T(4,128)} %copy.66), calls=%async_computation | async-start | bytes 131072 | tf_op jit(solution)/shard_map/all_to_all | solution.py:295
  138.6 26.6 %all-to-all-done = f32[6,4,32]{0,1,2:T(4,128)S(1)} async-done(((f32[6,4,32]{0,1,2:T(4,128)}), f32[6,4,32]{0,1,2:T(4,128)S(1)}, u32[]{:S(2)}, u32[]{:S(2)}) %all-to-all-start) | async-done | bytes 3104 | tf_op jit(solution)/shard_map/all_to_all | solution.py:295
  165.9 5.8 %unpack.8.rest_0_ = bf16[2,4,32,16384]{3,2,1,0:T(8,128)(2,1)} custom-call(s32[2]{0:T(128)} %pad_add_fusion.where, s32[32]{0:T(128)} %reshape.228.lengths, s32[32]{0:T(128)} %reshape.229.offsets, bf16[256,4,128]{2,1,0:T(4,128)(2,1)} %get-tuple-element.39.near, bf16[256,4,128]{2,1,0:T(4,128)(2,1)} %copy-done), custom_call_target="tpu_custom_call" | custom-call | flops 4194304 | bytes 1572864 | tf_op jit(solution)/shard_map/unpack/pallas_call | solution.py:204
  171.7 5.9 %unpack.9.rest_0_ = bf16[2,4,32,16384]{3,2,1,0:T(8,128)(2,1)} custom-call(s32[2]{0:T(128)} %pad_add_fusion.where, s32[32]{0:T(128)} %reshape.228.lengths, s32[32]{0:T(128)} %reshape.229.offsets, bf16[256,4,128]{2,1,0:T(4,128)(2,1)} %copy-done.5, bf16[256,4,128]{2,1,0:T(4,128)(2,1)} %copy-done.9, ...), custom_call_target="tpu_custom_call", output_to_operand_aliasing={{}: (5, {})} | custom-call | flops 4194304 | bytes 1572864 | tf_op jit(solution)/shard_map/unpack/pallas_call | solution.py:204
  177.6 5.8 %unpack.10.rest_0_ = bf16[2,4,32,16384]{3,2,1,0:T(8,128)(2,1)} custom-call(s32[2]{0:T(128)} %pad_add_fusion.where, s32[32]{0:T(128)} %reshape.228.lengths, s32[32]{0:T(128)} %reshape.229.offsets, bf16[256,4,128]{2,1,0:T(4,128)(2,1)} %copy-done.3, bf16[256,4,128]{2,1,0:T(4,128)(2,1)} %copy-done.4, ...), custom_call_target="tpu_custom_call", output_to_operand_aliasing={{}: (5, {})} | custom-call | flops 4194304 | bytes 1572864 | tf_op jit(solution)/shard_map/unpack/pallas_call | solution.py:204
  183.4 5.8 %unpack.11.rest_0_ = bf16[2,4,32,16384]{3,2,1,0:T(8,128)(2,1)} custom-call(s32[2]{0:T(128)} %pad_add_fusion.where, s32[32]{0:T(128)} %reshape.228.lengths, s32[32]{0:T(128)} %reshape.229.offsets, bf16[256,4,128]{2,1,0:T(4,128)(2,1)} %copy-done.1, bf16[256,4,128]{2,1,0:T(4,128)(2,1)} %copy-done.2, ...), custom_call_target="tpu_custom_call", output_to_operand_aliasing={{}: (5, {})} | custom-call | flops 4194304 | bytes 1572864 | tf_op jit(solution)/shard_map/unpack/pallas_call | solution.py:204
  189.2 5.8 %unpack.12.rest_0_ = bf16[2,4,32,16384]{3,2,1,0:T(8,128)(2,1)} custom-call(s32[2]{0:T(128)} %pad_add_fusion.where, s32[32]{0:T(128)} %reshape.228.lengths, s32[32]{0:T(128)} %reshape.229.offsets, bf16[256,4,128]{2,1,0:T(4,128)(2,1)} %get-tuple-element.30.near, bf16[256,4,128]{2,1,0:T(4,128)(2,1)} %copy-done.10, ...), custom_call_target="tpu_custom_call", output_to_operand_aliasing={{}: (5, {})} | custom-call | flops 4194304 | bytes 1572864 | tf_op jit(solution)/shard_map/unpack/pallas_call | solution.py:204
  195.1 5.9 %unpack.13.rest_0_ = bf16[2,4,32,16384]{3,2,1,0:T(8,128)(2,1)} custom-call(s32[2]{0:T(128)} %pad_add_fusion.where, s32[32]{0:T(128)} %reshape.228.lengths, s32[32]{0:T(128)} %reshape.229.offsets, bf16[256,4,128]{2,1,0:T(4,128)(2,1)} %copy-done.7, bf16[256,4,128]{2,1,0:T(4,128)(2,1)} %collective-permute-done.7.far, ...), custom_call_target="tpu_custom_call", output_to_operand_aliasing={{}: (5, {})} | custom-call | flops 4194304 | bytes 1572864 | tf_op jit(solution)/shard_map/unpack/pallas_call | solution.py:204
  202.3 5.8 %unpack.14.rest_0_ = bf16[2,4,32,16384]{3,2,1,0:T(8,128)(2,1)} custom-call(s32[2]{0:T(128)} %pad_add_fusion.where, s32[32]{0:T(128)} %reshape.228.lengths, s32[32]{0:T(128)} %reshape.229.offsets, bf16[256,4,128]{2,1,0:T(4,128)(2,1)} %copy-done.11, bf16[256,4,128]{2,1,0:T(4,128)(2,1)} %copy-done.12, ...), custom_call_target="tpu_custom_call", output_to_operand_aliasing={{}: (5, {})} | custom-call | flops 4194304 | bytes 1572864 | tf_op jit(solution)/shard_map/unpack/pallas_call | solution.py:204
  209.5 5.8 %unpack.15 = bf16[2,4,32,16384]{3,2,1,0:T(8,128)(2,1)} custom-call(s32[2]{0:T(128)} %pad_add_fusion.where, s32[32]{0:T(128)} %reshape.228.lengths, s32[32]{0:T(128)} %reshape.229.offsets, bf16[256,4,128]{2,1,0:T(4,128)(2,1)} %copy-done.6, bf16[256,4,128]{2,1,0:T(4,128)(2,1)} %copy-done.8, ...), custom_call_target="tpu_custom_call", output_to_operand_aliasing={{}: (5, {})} | custom-call | flops 4194304 | bytes 1572864 | tf_op jit(solution)/shard_map/unpack/pallas_call | solution.py:204
  (83 shorter events, 15.4 us)
Async XLA Ops:
  1.3 16.6 %collective-permute-start.1 = (f32[8,128]{1,0:T(8,128)S(1)}, f32[8,128]{1,0:T(8,128)S(1)}, u32[]{:S(2)}, u32[]{:S(2)}) collective-permute-start(f32[8,128]{1,0:T(8,128)S(1)} %bitcast.79), channel_id=1, source_target_pairs={{4,0},{8,4},{12,8},{16,12},{20,16},{24,20},{28,24},{5,1},{9,5},{13... | collective-permute-start | bytes 12296 | tf_op jit(solution)/shard_map/ppermute | solution.py:238
  2.6 15.4 %collective-permute-start = (f32[8,128]{1,0:T(8,128)S(1)}, f32[8,128]{1,0:T(8,128)S(1)}, u32[]{:S(2)}, u32[]{:S(2)}) collective-permute-start(f32[8,128]{1,0:T(8,128)S(1)} %bitcast.78), channel_id=1, source_target_pairs={{0,4},{4,8},{8,12},{12,16},{16,20},{20,24},{24,28},{1,5},{5,9},{9,... | collective-permute-start | bytes 12296 | tf_op jit(solution)/shard_map/ppermute | solution.py:238
  60.9 14.1 %collective-permute-start.9 = (bf16[256,4,128]{2,1,0:T(4,128)(2,1)}, bf16[256,4,128]{2,1,0:T(4,128)(2,1)S(1)}, u32[]{:S(2)}, u32[]{:S(2)}) collective-permute-start(bf16[256,4,128]{2,1,0:T(4,128)(2,1)} %get-tuple-element.33), channel_id=1, source_target_pairs={{0,24},{4,28},{8,16},{12,20},{16,8},{20,12},{24,0},{28,4},{1,25},{... | collective-permute-start | bytes 786440 | tf_op jit(solution)/shard_map/ppermute | solution.py:283
  65.1 30.9 %collective-permute-start.10 = (bf16[256,4,128]{2,1,0:T(4,128)(2,1)}, bf16[256,4,128]{2,1,0:T(4,128)(2,1)S(1)}, u32[]{:S(2)}, u32[]{:S(2)}) collective-permute-start(bf16[256,4,128]{2,1,0:T(4,128)(2,1)} %get-tuple-element.34), channel_id=1, source_target_pairs={{0,28},{4,24},{8,20},{12,16},{16,12},{20,8},{24,4},{28,0},{1,29},{... | collective-permute-start | bytes 786440 | tf_op jit(solution)/shard_map/ppermute | solution.py:283
  67.2 37.8 %collective-permute-start.11 = (bf16[256,4,128]{2,1,0:T(4,128)(2,1)}, bf16[256,4,128]{2,1,0:T(4,128)(2,1)S(1)}, u32[]{:S(2)}, u32[]{:S(2)}) collective-permute-start(bf16[256,4,128]{2,1,0:T(4,128)(2,1)} %get-tuple-element.35), channel_id=1, source_target_pairs={{0,16},{4,20},{8,24},{12,28},{16,0},{20,4},{24,8},{28,12},{1,17},{... | collective-permute-start | bytes 786440 | tf_op jit(solution)/shard_map/ppermute | solution.py:283
  68.0 46.2 %collective-permute-start.12 = (bf16[256,4,128]{2,1,0:T(4,128)(2,1)}, bf16[256,4,128]{2,1,0:T(4,128)(2,1)S(1)}, u32[]{:S(2)}, u32[]{:S(2)}) collective-permute-start(bf16[256,4,128]{2,1,0:T(4,128)(2,1)} %get-tuple-element.36), channel_id=1, source_target_pairs={{0,20},{4,16},{8,28},{12,24},{16,4},{20,0},{24,12},{28,8},{1,21},{... | collective-permute-start | bytes 786440 | tf_op jit(solution)/shard_map/ppermute | solution.py:283
  73.6 40.5 %collective-permute-start.13 = (bf16[256,4,128]{2,1,0:T(4,128)(2,1)}, bf16[256,4,128]{2,1,0:T(4,128)(2,1)S(1)}, u32[]{:S(2)}, u32[]{:S(2)}) collective-permute-start(bf16[256,4,128]{2,1,0:T(4,128)(2,1)} %get-tuple-element.37), channel_id=1, source_target_pairs={{0,8},{4,12},{8,0},{12,4},{16,24},{20,28},{24,16},{28,20},{1,9},{5... | collective-permute-start | bytes 786440 | tf_op jit(solution)/shard_map/ppermute | solution.py:283
  75.0 108.4 %copy-start.1 = (bf16[256,4,128]{2,1,0:T(4,128)(2,1)}, bf16[256,4,128]{2,1,0:T(4,128)(2,1)S(1)}, u32[]{:S(2)}) copy-start(bf16[256,4,128]{2,1,0:T(4,128)(2,1)S(1)} %collective-permute-done.9.near) | copy-start | bytes 786436
  75.0 41.6 %collective-permute-start.14 = (bf16[256,4,128]{2,1,0:T(4,128)(2,1)}, bf16[256,4,128]{2,1,0:T(4,128)(2,1)S(1)}, u32[]{:S(2)}, u32[]{:S(2)}) collective-permute-start(bf16[256,4,128]{2,1,0:T(4,128)(2,1)} %get-tuple-element.38), channel_id=1, source_target_pairs={{0,12},{4,8},{8,4},{12,0},{16,28},{20,24},{24,20},{28,16},{1,13},{... | collective-permute-start | bytes 786440 | tf_op jit(solution)/shard_map/ppermute | solution.py:283
  96.0 87.4 %copy-start.2 = (bf16[256,4,128]{2,1,0:T(4,128)(2,1)}, bf16[256,4,128]{2,1,0:T(4,128)(2,1)S(1)}, u32[]{:S(2)}) copy-start(bf16[256,4,128]{2,1,0:T(4,128)(2,1)S(1)} %collective-permute-done.10.far) | copy-start | bytes 786436
  96.0 23.5 %collective-permute-start.15 = (bf16[256,4,128]{2,1,0:T(4,128)(2,1)}, bf16[256,4,128]{2,1,0:T(4,128)(2,1)S(1)}, u32[]{:S(2)}, u32[]{:S(2)}) collective-permute-start(bf16[256,4,128]{2,1,0:T(4,128)(2,1)} %get-tuple-element.40), channel_id=1, source_target_pairs={{0,4},{4,0},{8,12},{12,8},{16,20},{20,16},{24,28},{28,24},{1,5},{5... | collective-permute-start | bytes 786440 | tf_op jit(solution)/shard_map/ppermute | solution.py:283
  105.0 72.6 %copy-start.3 = (bf16[256,4,128]{2,1,0:T(4,128)(2,1)}, bf16[256,4,128]{2,1,0:T(4,128)(2,1)S(1)}, u32[]{:S(2)}) copy-start(bf16[256,4,128]{2,1,0:T(4,128)(2,1)S(1)} %collective-permute-done.11.near) | copy-start | bytes 786436
  105.0 14.6 %collective-permute-start.6 = (bf16[256,4,128]{2,1,0:T(4,128)(2,1)}, bf16[256,4,128]{2,1,0:T(4,128)(2,1)S(1)}, u32[]{:S(2)}, u32[]{:S(2)}) collective-permute-start(bf16[256,4,128]{2,1,0:T(4,128)(2,1)} %get-tuple-element.28), channel_id=1, source_target_pairs={{0,8},{4,12},{8,0},{12,4},{16,24},{20,28},{24,16},{28,20},{1,9},{5... | collective-permute-start | bytes 786440 | tf_op jit(solution)/shard_map/ppermute | solution.py:283
  114.1 63.4 %copy-start.4 = (bf16[256,4,128]{2,1,0:T(4,128)(2,1)}, bf16[256,4,128]{2,1,0:T(4,128)(2,1)S(1)}, u32[]{:S(2)}) copy-start(bf16[256,4,128]{2,1,0:T(4,128)(2,1)S(1)} %collective-permute-done.12.far) | copy-start | bytes 786436
  114.2 7.8 %collective-permute-start.8 = (bf16[256,4,128]{2,1,0:T(4,128)(2,1)}, bf16[256,4,128]{2,1,0:T(4,128)(2,1)S(1)}, u32[]{:S(2)}, u32[]{:S(2)}) collective-permute-start(bf16[256,4,128]{2,1,0:T(4,128)(2,1)} %get-tuple-element.31), channel_id=1, source_target_pairs={{0,4},{4,0},{8,12},{12,8},{16,20},{20,16},{24,28},{28,24},{1,5},{5... | collective-permute-start | bytes 786440 | tf_op jit(solution)/shard_map/ppermute | solution.py:283
  114.2 57.5 %copy-start.5 = (bf16[256,4,128]{2,1,0:T(4,128)(2,1)}, bf16[256,4,128]{2,1,0:T(4,128)(2,1)S(1)}, u32[]{:S(2)}) copy-start(bf16[256,4,128]{2,1,0:T(4,128)(2,1)S(1)} %collective-permute-done.13.near) | copy-start | bytes 786436
  114.2 93.9 %collective-permute-start.2 = (bf16[256,4,128]{2,1,0:T(4,128)(2,1)}, bf16[256,4,128]{2,1,0:T(4,128)(2,1)S(1)}, u32[]{:S(2)}, u32[]{:S(2)}) collective-permute-start(bf16[256,4,128]{2,1,0:T(4,128)(2,1)} %get-tuple-element.24), channel_id=1, source_target_pairs={{0,24},{4,28},{8,16},{12,20},{16,8},{20,12},{24,0},{28,4},{1,25},{... | collective-permute-start | bytes 786440 | tf_op jit(solution)/shard_map/ppermute | solution.py:283
  116.6 55.0 %copy-start.9 = (bf16[256,4,128]{2,1,0:T(4,128)(2,1)}, bf16[256,4,128]{2,1,0:T(4,128)(2,1)S(1)}, u32[]{:S(2)}) copy-start(bf16[256,4,128]{2,1,0:T(4,128)(2,1)S(1)} %collective-permute-done.14.far) | copy-start | bytes 786436
  116.7 91.5 %collective-permute-start.3 = (bf16[256,4,128]{2,1,0:T(4,128)(2,1)}, bf16[256,4,128]{2,1,0:T(4,128)(2,1)S(1)}, u32[]{:S(2)}, u32[]{:S(2)}) collective-permute-start(bf16[256,4,128]{2,1,0:T(4,128)(2,1)} %get-tuple-element.25), channel_id=1, source_target_pairs={{0,28},{4,24},{8,20},{12,16},{16,12},{20,8},{24,4},{28,0},{1,29},{... | collective-permute-start | bytes 786440 | tf_op jit(solution)/shard_map/ppermute | solution.py:283
  119.5 46.3 %copy-start = (bf16[256,4,128]{2,1,0:T(4,128)(2,1)}, bf16[256,4,128]{2,1,0:T(4,128)(2,1)S(1)}, u32[]{:S(2)}) copy-start(bf16[256,4,128]{2,1,0:T(4,128)(2,1)S(1)} %collective-permute-done.15.far) | copy-start | bytes 786436
  119.5 81.4 %collective-permute-start.4 = (bf16[256,4,128]{2,1,0:T(4,128)(2,1)}, bf16[256,4,128]{2,1,0:T(4,128)(2,1)S(1)}, u32[]{:S(2)}, u32[]{:S(2)}) collective-permute-start(bf16[256,4,128]{2,1,0:T(4,128)(2,1)} %get-tuple-element.26), channel_id=1, source_target_pairs={{0,16},{4,20},{8,24},{12,28},{16,0},{20,4},{24,8},{28,12},{1,17},{... | collective-permute-start | bytes 786440 | tf_op jit(solution)/shard_map/ppermute | solution.py:283
  119.6 58.0 %copy-start.7 = (bf16[256,4,128]{2,1,0:T(4,128)(2,1)}, bf16[256,4,128]{2,1,0:T(4,128)(2,1)S(1)}, u32[]{:S(2)}) copy-start(bf16[256,4,128]{2,1,0:T(4,128)(2,1)S(1)} %collective-permute-done.6.near) | copy-start | bytes 786436
  119.6 81.4 %collective-permute-start.5 = (bf16[256,4,128]{2,1,0:T(4,128)(2,1)}, bf16[256,4,128]{2,1,0:T(4,128)(2,1)S(1)}, u32[]{:S(2)}, u32[]{:S(2)}) collective-permute-start(bf16[256,4,128]{2,1,0:T(4,128)(2,1)} %get-tuple-element.27), channel_id=1, source_target_pairs={{0,20},{4,16},{8,28},{12,24},{16,4},{20,0},{24,12},{28,8},{1,21},{... | collective-permute-start | bytes 786440 | tf_op jit(solution)/shard_map/ppermute | solution.py:283
  121.9 55.6 %copy-start.10 = (bf16[256,4,128]{2,1,0:T(4,128)(2,1)}, bf16[256,4,128]{2,1,0:T(4,128)(2,1)S(1)}, u32[]{:S(2)}) copy-start(bf16[256,4,128]{2,1,0:T(4,128)(2,1)S(1)} %collective-permute-done.8.far) | copy-start | bytes 786436
  121.9 73.1 %collective-permute-start.7 = (bf16[256,4,128]{2,1,0:T(4,128)(2,1)}, bf16[256,4,128]{2,1,0:T(4,128)(2,1)}, u32[]{:S(2)}, u32[]{:S(2)}) collective-permute-start(bf16[256,4,128]{2,1,0:T(4,128)(2,1)} %get-tuple-element.29), channel_id=1, source_target_pairs={{0,12},{4,8},{8,4},{12,0},{16,28},{20,24},{24,20},{28,16},{1,13},{... | collective-permute-start | bytes 786440 | tf_op jit(solution)/shard_map/ppermute | solution.py:283
  129.6 35.6 %all-to-all-start = ((f32[6,4,32]{0,1,2:T(4,128)}), f32[6,4,32]{0,1,2:T(4,128)S(1)}, u32[]{:S(2)}, u32[]{:S(2)}) async-start(f32[6,4,32]{0,1,2:T(4,128)} %copy.66), calls=%async_computation | async-start | bytes 131072 | tf_op jit(solution)/shard_map/all_to_all | solution.py:295
  200.9 0.7 copy-start.11
  201.6 0.7 copy-start.12
  208.1 0.7 copy-start.6
  208.8 0.7 copy-start.8

commit v3 on v2

--- a/solution.py
+++ b/solution.py
@@ -51,7 +51,7 @@
             power[pl.ds(at, SUB)] = (weight * (f_re * f_re + f_im * f_im)).astype(jnp.bfloat16)
             return carry
 
-        lax.fori_loop(0, TABLE // SUB, inner, 0)
+        lax.fori_loop(0, TABLE // SUB, inner, 0, unroll=2)
 
 
 def heterodyne(strain, fid, psd, halo, cos_t, sin_t, cos_s, sin_s):
@@ -129,39 +129,62 @@
     )(real, imag, power, first, length)
 
 
-def pack_kernel(starts, lengths, offsets, prod, *rest):
-    *packed, sem = rest
-    pair = starts.shape[0] // len(packed)
-
-    def copies():
-        for step, target in enumerate(packed):
-            for rank in range(pair):
-                j = step * pair + rank
-                n = lengths[j]
-                yield pltpu.make_async_copy(
-                    prod.at[pl.ds(starts[j], n)], target.at[pl.ds(offsets[j], n)], sem.at[j]
-                )
-
-    for copy in copies():
-        copy.start()
-    for copy in copies():
-        copy.wait()
-
-
-def pack(starts, lengths, offsets, prod, groups, span):
+def pack_kernel(lengths, owners, prod, *rest):
+    *packed, first, size, offset, count, filled, sem = rest
+    groups, bins = lengths.shape
+    pair = bins // groups
+    me = lax.axis_index("freq")
+    span = packed[0].shape[0]
+
+    def clear(p, carry):
+        count[p] = 0
+        filled[p] = 0
+        return carry
+
+    lax.fori_loop(0, groups, clear, 0)
+
+    def place(j, start):
+        step = owners[me, j] ^ me
+        n = lengths[me, j]
+        slot = step * pair + count[step]
+        first[slot] = start
+        size[slot] = n
+        offset[slot] = filled[step]
+        count[step] = count[step] + 1
+        filled[step] = filled[step] + n
+        return start + n
+
+    lax.fori_loop(0, bins, place, jnp.int32(0))
+
+    order = list(range(groups // 2, groups)) + list(range(groups // 2))
+    for step in order:
+        for rank in range(pair):
+            j = step * pair + rank
+            n = size[j]
+            pltpu.make_async_copy(
+                prod.at[pl.ds(first[j], n)], packed[step].at[pl.ds(offset[j], n)], sem.at[step]
+            ).start()
+    for step in order:
+        pltpu.make_async_copy(prod.at[pl.ds(0, span)], packed[step], sem.at[step]).wait()
+
+
+def pack(lengths, owners, prod, span):
+    groups, bins = lengths.shape
     shape = jax.ShapeDtypeStruct((span,) + prod.shape[1:], jnp.bfloat16)
     return pl.pallas_call(
         pack_kernel,
         grid_spec=pltpu.PrefetchScalarGridSpec(
-            num_scalar_prefetch=3,
+            num_scalar_prefetch=2,
             in_specs=[pl.BlockSpec(memory_space=pltpu.VMEM)],
             out_specs=[pl.BlockSpec(memory_space=pl.ANY)] * groups,
-            scratch_shapes=[pltpu.SemaphoreType.DMA((starts.shape[0],))],
+            scratch_shapes=[pltpu.SMEM((bins,), jnp.int32)] * 3
+            + [pltpu.SMEM((groups,), jnp.int32)] * 2
+            + [pltpu.SemaphoreType.DMA((groups,))],
         ),
         out_shape=[shape] * groups,
         cost_estimate=pl.CostEstimate(flops=0, bytes_accessed=4 * prod.size, transcendentals=0),
         name="pack",
-    )(starts, lengths, offsets, prod)
+    )(lengths, owners, prod)
 
 
 def unpack_kernel(chunk, pair, unit, where, lengths, offsets, near, far, *rest):
@@ -177,7 +200,12 @@
             base = offsets[j] + m0
             lane = base_slot + rank
 
-            @pl.when(n > 0)
+            @pl.when(n >= chunk)
+            def _(got=got, base=base, lane=lane):
+                for m in range(chunk):
+                    work[m, pl.ds(lane, rows, stride=slots)] = got[base + m].astype(jnp.float32)
+
+            @pl.when(jnp.logical_and(n > 0, n < chunk))
             def _(got=got, n=n, base=base, lane=lane):
                 for m in range(chunk):
                     value = got[jnp.minimum(base + m, span - 1)].astype(jnp.float32)
@@ -250,6 +278,16 @@
         jnp.cos(inside), jnp.sin(inside), spread(jnp.cos(outer)), spread(jnp.sin(outer)),
     )
 
+    steps = list(range(n_freq // 2, n_freq)) + list(range(1, n_freq // 2))
+    got = []
+    for values in (real, imag):
+        packed = pack(bin_blocks, bin_owner, values.reshape(blocks, rows, LANES), span)
+        here = {0: packed[0]}
+        for s in steps:
+            here[s] = lax.ppermute(packed[s], "freq", [(i, i ^ s) for i in range(n_freq)])
+        got.append(here)
+
+    bin_blocks, bin_owner, got[1][0] = lax.optimization_barrier((bin_blocks, bin_owner, got[1][0]))
     position = jnp.arange(bins, dtype=jnp.int32)
     earlier = (position[None, :] < position[:, None])[None]
     same = bin_owner[:, :, None] == bin_owner[:, None, :]
@@ -258,13 +296,11 @@
     ranks = jnp.sum(both.astype(jnp.int32), axis=2)
     offsets = jnp.sum(jnp.where(both, bin_blocks[:, None, :], 0), axis=2)
     at_me = lambda a: lax.dynamic_index_in_dim(a, me, 0, keepdims=False)
-    my_start, my_len, my_owner, my_off, my_rank = map(at_me, (starts, bin_blocks, bin_owner, offsets, ranks))
+    my_start, my_len, my_owner, _, my_rank = map(at_me, (starts, bin_blocks, bin_owner, offsets, ranks))
 
     pick = lambda key, values: jnp.sum(
         jnp.where(key[None, :] == position[:, None], values[None, :], 0), axis=1
     )
-    by_step = (my_owner ^ me) * pair + my_rank
-    send_start, send_len, send_off = (pick(by_step, v) for v in (my_start, my_len, my_off))
     peers = jnp.arange(n_freq, dtype=jnp.int32) ^ me
     to_me = jnp.logical_and(
         (bin_owner == me)[:, None, :], ranks[:, None, :] == jnp.arange(pair, dtype=jnp.int32)[None, :, None]
@@ -273,15 +309,6 @@
     in_len = jnp.sum(jnp.where(to_me, bin_blocks[None, :, None, :], 0), axis=(1, 3)).reshape(-1)
     in_off = jnp.sum(jnp.where(to_me, offsets[None, :, None, :], 0), axis=(1, 3)).reshape(-1)
     where = jnp.stack([me // 2, me % 2]).astype(jnp.int32)
-
-    steps = list(range(n_freq // 2, n_freq)) + list(range(1, n_freq // 2))
-    got = []
-    for values in (real, imag):
-        packed = pack(send_start, send_len, send_off, values.reshape(blocks, rows, LANES), n_freq, span)
-        here = {0: packed[0]}
-        for s in steps:
-            here[s] = lax.ppermute(packed[s], "freq", [(i, i ^ s) for i in range(n_freq)])
-        got.append(here)
 
     my_slot = my_owner * pair + my_rank
     slot_first, slot_len = pick(my_slot, my_start), pick(my_slot, my_len)

time: 216 us -> 185 us (0.86)
  Pallas kernels: 90.6 us -> 77.2 us
  waiting for transfers between devices: 44.3 us -> 33.3 us
  starting transfers between devices: 59.4 us -> 55.5 us
  other arithmetic: 9.42 us -> 5.96 us
    all_to_all x1, waiting for transfers between devices: 26.6 us -> 14.2 us  [local(): lax.all_to_all(local_summary, 'freq', split_axis=2, concat_axis=2, tiled=...]
    pallas_call x1, Pallas kernels: 25.7 us -> 15.8 us  [heterodyne(): pl.pallas_call(het_kernel, grid=(steps,), in_specs=[pl.BlockSpec((2, rows...]
    pallas_call x8, Pallas kernels: 46.7 us -> 43.2 us  [unpack(): pl.pallas_call(functools.partial(unpack_kernel, chunk, pair, unit), grid_...]
  transfers between devices with their start and end apart: 17 -> 17, of which waited for: 3 -> 4; matrix products, arithmetic and copies ran while one was open for 6% -> 5% of each run, Pallas kernels for 21% -> 21%
where the time goes in v3:
time: 185 us; the launch traced here: 184 us
  Pallas kernels  77.2 us (42%)
  starting transfers between devices  55.5 us (30%)
  waiting for transfers between devices  33.3 us (18%)
  local copies, waits for them, and re-layouts  10.9 us (6%)
  other arithmetic  5.96 us (3%)
    ppermute x14, starting transfers between devices, local(): lax.ppermute(packed[s], 'freq', [(i, i ^ s) for i in range(n_freq)])  43.5 us
    pallas_call x8, Pallas kernels, unpack(): pl.pallas_call(functools.partial(unpack_kernel, chunk, pair, unit), grid_...  43.2 us
    ppermute x14, waiting for transfers between devices, local(): lax.ppermute(packed[s], 'freq', [(i, i ^ s) for i in range(n_freq)])  19.1 us
    pallas_call x1, Pallas kernels, heterodyne(): pl.pallas_call(het_kernel, grid=(steps,), in_specs=[pl.BlockSpec((2, rows...  15.8 us
    all_to_all x1, waiting for transfers between devices, local(): lax.all_to_all(local_summary, 'freq', split_axis=2, concat_axis=2, tiled=...  14.2 us
    pallas_call x1, Pallas kernels, bin_sums(): pl.pallas_call(functools.partial(sums_kernel, tmpl_rows), grid=(total //...  10.5 us
    pallas_call x2, Pallas kernels, pack(): pl.pallas_call(pack_kernel, grid_spec=pltpu.PrefetchScalarGridSpec(num_sc...  7.65 us
    ppermute x1, starting transfers between devices, local(): lax.ppermute(psd_v[-8:], 'freq', up)  5.5 us
  transfers between devices with their start and end apart: 17, of which 4 were waited for; matrix products, arithmetic and copies ran while one was open for 5% of the time, Pallas kernels for 21%

profile of v3, /device:TPU:0, one launch (start us, length us, event | category | flops | bytes accessed | tf_op | source)
XLA Modules:
  0.0 183.7 jit_solution(4123584578795919849)
XLA Ops:
  1.3 1.3 collective-permute-start.1
  2.6 5.5 %collective-permute-start = (f32[8,128]{1,0:T(8,128)S(1)}, f32[8,128]{1,0:T(8,128)S(1)}, u32[]{:S(2)}, u32[]{:S(2)}) collective-permute-start(f32[8,128]{1,0:T(8,128)S(1)} %bitcast.74), channel_id=1, source_target_pairs={{0,4},{4,8},{8,12},{12,16},{16,20},{20,24},{24,28},{1,5},{5,9},{9,... | collective-permute-start | bytes 12296 | tf_op jit(solution)/shard_map/ppermute | solution.py:266
  9.1 0.8 fusion.10
  9.9 1.3 multiply_sine_fusion
  14.0 15.8 %heterodyne.1 = (bf16[8192,128]{1,0:T(8,128)(2,1)}, bf16[8192,128]{1,0:T(8,128)(2,1)}, bf16[8192,128]{1,0:T(8,128)(2,1)}) custom-call(bf16[2,8192,128]{2,1,0:T(8,128)(2,1)} %bitcast.68, bf16[2,8192,128]{2,1,0:T(8,128)(2,1)} %bitcast.69, f32[8192,128]{1,0:T(8,128)} %bitcast.63, f32[8192,128]{1,0:T(8,128)} %bitcast.64, f32[8192,128]{1,0:T(8,128)} %bitcast.65, ...), custom_call_target="tpu_custom_call" | custom-call | flops 62914560 | bytes 18874368 | tf_op jit(solution)/shard_map/heterodyne/pallas_call | solution.py:62
  29.8 3.9 %pack.2 = (bf16[256,4,128]{2,1,0:T(4,128)(2,1)}, bf16[256,4,128]{2,1,0:T(4,128)(2,1)}, bf16[256,4,128]{2,1,0:T(4,128)(2,1)}, bf16[256,4,128]{2,1,0:T(4,128)(2,1)...) custom-call(s32[8,32]{1,0:T(8,128)} %lengths.3, ...), custom_call_target="tpu_custom_call" | custom-call | bytes 4194304 | tf_op jit(solution)/shard_map/pack/pallas_call | solution.py:174
  35.7 10.5 %sums.1 = (f32[8,128]{1,0:T(8,128)}, f32[8,128]{1,0:T(8,128)}) custom-call(bf16[8192,128]{1,0:T(8,128)(2,1)} %get-tuple-element.38.real, bf16[8192,128]{1,0:T(8,128)(2,1)} %get-tuple-element.26.imag, bf16[8192,128]{1,0:T(8,128)(2,1)} %get-tuple-element.47.power, s32[1,128]{1,0:T(1,128)} %broadcast_in_dim_tile.8.first, s32[1,128]{1,0:T(1,128)} %broadcast_in_dim_tile.9.length), custom_call_target="tpu_custom_call" | custom-call | flops 209715200 | bytes 6291456 | tf_op jit(solution)/shard_map/sums/pallas_call | solution.py:121
  47.0 3.8 %pack.3 = (bf16[256,4,128]{2,1,0:T(4,128)(2,1)}, bf16[256,4,128]{2,1,0:T(4,128)(2,1)}, bf16[256,4,128]{2,1,0:T(4,128)(2,1)}, bf16[256,4,128]{2,1,0:T(4,128)(2,1)...) custom-call(s32[8,32]{1,0:T(8,128)} %lengths.3, ...), custom_call_target="tpu_custom_call" | custom-call | bytes 4194304 | tf_op jit(solution)/shard_map/pack/pallas_call | solution.py:174
  50.8 4.3 %collective-permute-start.9 = (bf16[256,4,128]{2,1,0:T(4,128)(2,1)}, bf16[256,4,128]{2,1,0:T(4,128)(2,1)S(1)}, u32[]{:S(2)}, u32[]{:S(2)}) collective-permute-start(bf16[256,4,128]{2,1,0:T(4,128)(2,1)} %get-tuple-element.39), channel_id=1, source_target_pairs={{0,24},{4,28},{8,16},{12,20},{16,8},{20,12},{24,0},{28,4},{1,25},{... | collective-permute-start | bytes 786440 | tf_op jit(solution)/shard_map/ppermute | solution.py:287
  55.1 2.0 %collective-permute-start.10 = (bf16[256,4,128]{2,1,0:T(4,128)(2,1)}, bf16[256,4,128]{2,1,0:T(4,128)(2,1)S(1)}, u32[]{:S(2)}, u32[]{:S(2)}) collective-permute-start(bf16[256,4,128]{2,1,0:T(4,128)(2,1)} %get-tuple-element.40), channel_id=1, source_target_pairs={{0,28},{4,24},{8,20},{12,16},{16,12},{20,8},{24,4},{28,0},{1,29},{... | collective-permute-start | bytes 786440 | tf_op jit(solution)/shard_map/ppermute | solution.py:287
  57.0 0.8 collective-permute-start.11
  57.8 1.1 collective-permute-start.12
  59.0 1.4 collective-permute-start.13
  61.1 1.5 collective-permute-done.9.near
  62.6 23.2 %collective-permute-start.14 = (bf16[256,4,128]{2,1,0:T(4,128)(2,1)}, bf16[256,4,128]{2,1,0:T(4,128)(2,1)S(1)}, u32[]{:S(2)}, u32[]{:S(2)}) collective-permute-start(bf16[256,4,128]{2,1,0:T(4,128)(2,1)} %get-tuple-element.44), channel_id=1, source_target_pairs={{0,12},{4,8},{8,4},{12,0},{16,28},{20,24},{24,20},{28,16},{1,13},{... | collective-permute-start | bytes 786440 | tf_op jit(solution)/shard_map/ppermute | solution.py:287
  85.8 9.0 %collective-permute-done.11.near = bf16[256,4,128]{2,1,0:T(4,128)(2,1)S(1)} collective-permute-done((bf16[256,4,128]{2,1,0:T(4,128)(2,1)}, bf16[256,4,128]{2,1,0:T(4,128)(2,1)S(1)}, u32[]{:S(2)}, u32[]{:S(2)}) %collective-permute-start.11) | collective-permute-done | bytes 262176 | tf_op jit(solution)/shard_map/ppermute | solution.py:287
  95.4 8.6 %collective-permute-done.12.far = bf16[256,4,128]{2,1,0:T(4,128)(2,1)S(1)} collective-permute-done((bf16[256,4,128]{2,1,0:T(4,128)(2,1)}, bf16[256,4,128]{2,1,0:T(4,128)(2,1)S(1)}, u32[]{:S(2)}, u32[]{:S(2)}) %collective-permute-start.12) | collective-permute-done | bytes 262176 | tf_op jit(solution)/shard_map/ppermute | solution.py:287
  104.8 5.2 %all-to-all-start = ((f32[6,4,32]{0,1,2:T(4,128)}), f32[6,4,32]{0,1,2:T(4,128)S(1)}, u32[]{:S(2)}, u32[]{:S(2)}) async-start(f32[6,4,32]{0,1,2:T(4,128)} %copy.66), calls=%async_computation | async-start | bytes 131072 | tf_op jit(solution)/shard_map/all_to_all | solution.py:322
  110.0 3.9 %collective-permute-start.2 = (bf16[256,4,128]{2,1,0:T(4,128)(2,1)}, bf16[256,4,128]{2,1,0:T(4,128)(2,1)S(1)}, u32[]{:S(2)}, u32[]{:S(2)}) collective-permute-start(bf16[256,4,128]{2,1,0:T(4,128)(2,1)} %get-tuple-element.30), channel_id=1, source_target_pairs={{0,24},{4,28},{8,16},{12,20},{16,8},{20,12},{24,0},{28,4},{1,25},{... | collective-permute-start | bytes 786440 | tf_op jit(solution)/shard_map/ppermute | solution.py:287
  113.9 1.5 collective-permute-start.3
  115.9 1.9 %collective-permute-start.5 = (bf16[256,4,128]{2,1,0:T(4,128)(2,1)}, bf16[256,4,128]{2,1,0:T(4,128)(2,1)S(1)}, u32[]{:S(2)}, u32[]{:S(2)}) collective-permute-start(bf16[256,4,128]{2,1,0:T(4,128)(2,1)} %get-tuple-element.33), channel_id=1, source_target_pairs={{0,20},{4,16},{8,28},{12,24},{16,4},{20,0},{24,12},{28,8},{1,21},{... | collective-permute-start | bytes 786440 | tf_op jit(solution)/shard_map/ppermute | solution.py:287
  117.8 2.4 %collective-permute-start.7 = (bf16[256,4,128]{2,1,0:T(4,128)(2,1)}, bf16[256,4,128]{2,1,0:T(4,128)(2,1)}, u32[]{:S(2)}, u32[]{:S(2)}) collective-permute-start(bf16[256,4,128]{2,1,0:T(4,128)(2,1)} %get-tuple-element.35), channel_id=1, source_target_pairs={{0,12},{4,8},{8,4},{12,0},{16,28},{20,24},{24,20},{28,16},{1,13},{... | collective-permute-start | bytes 786440 | tf_op jit(solution)/shard_map/ppermute | solution.py:287
  120.2 1.3 fusion.1
  122.7 14.2 %all-to-all-done = f32[6,4,32]{0,1,2:T(4,128)S(1)} async-done(((f32[6,4,32]{0,1,2:T(4,128)}), f32[6,4,32]{0,1,2:T(4,128)S(1)}, u32[]{:S(2)}, u32[]{:S(2)}) %all-to-all-start) | async-done | bytes 3104 | tf_op jit(solution)/shard_map/all_to_all | solution.py:322
  137.7 5.4 %unpack.8.rest_0_ = bf16[2,4,32,16384]{3,2,1,0:T(8,128)(2,1)} custom-call(s32[2]{0:T(128)} %pad_add_fusion.where, s32[32]{0:T(128)} %reshape.235.lengths, s32[32]{0:T(128)} %reshape.236.offsets, bf16[256,4,128]{2,1,0:T(4,128)(2,1)} %get-tuple-element.45.near, bf16[256,4,128]{2,1,0:T(4,128)(2,1)} %copy-done), custom_call_target="tpu_custom_call" | custom-call | flops 4194304 | bytes 1572864 | tf_op jit(solution)/shard_map/unpack/pallas_call | solution.py:232
  143.1 5.4 %unpack.9.rest_0_ = bf16[2,4,32,16384]{3,2,1,0:T(8,128)(2,1)} custom-call(s32[2]{0:T(128)} %pad_add_fusion.where, s32[32]{0:T(128)} %reshape.235.lengths, s32[32]{0:T(128)} %reshape.236.offsets, bf16[256,4,128]{2,1,0:T(4,128)(2,1)} %copy-done.5, bf16[256,4,128]{2,1,0:T(4,128)(2,1)} %copy-done.7, ...), custom_call_target="tpu_custom_call", output_to_operand_aliasing={{}: (5, {})} | custom-call | flops 4194304 | bytes 1572864 | tf_op jit(solution)/shard_map/unpack/pallas_call | solution.py:232
  148.5 5.4 %unpack.10.rest_0_ = bf16[2,4,32,16384]{3,2,1,0:T(8,128)(2,1)} custom-call(s32[2]{0:T(128)} %pad_add_fusion.where, s32[32]{0:T(128)} %reshape.235.lengths, s32[32]{0:T(128)} %reshape.236.offsets, bf16[256,4,128]{2,1,0:T(4,128)(2,1)} %copy-done.3, bf16[256,4,128]{2,1,0:T(4,128)(2,1)} %copy-done.4, ...), custom_call_target="tpu_custom_call", output_to_operand_aliasing={{}: (5, {})} | custom-call | flops 4194304 | bytes 1572864 | tf_op jit(solution)/shard_map/unpack/pallas_call | solution.py:232
  153.9 5.4 %unpack.11.rest_0_ = bf16[2,4,32,16384]{3,2,1,0:T(8,128)(2,1)} custom-call(s32[2]{0:T(128)} %pad_add_fusion.where, s32[32]{0:T(128)} %reshape.235.lengths, s32[32]{0:T(128)} %reshape.236.offsets, bf16[256,4,128]{2,1,0:T(4,128)(2,1)} %copy-done.1, bf16[256,4,128]{2,1,0:T(4,128)(2,1)} %copy-done.2, ...), custom_call_target="tpu_custom_call", output_to_operand_aliasing={{}: (5, {})} | custom-call | flops 4194304 | bytes 1572864 | tf_op jit(solution)/shard_map/unpack/pallas_call | solution.py:232
  159.3 5.4 %unpack.12.rest_0_ = bf16[2,4,32,16384]{3,2,1,0:T(8,128)(2,1)} custom-call(s32[2]{0:T(128)} %pad_add_fusion.where, s32[32]{0:T(128)} %reshape.235.lengths, s32[32]{0:T(128)} %reshape.236.offsets, bf16[256,4,128]{2,1,0:T(4,128)(2,1)} %get-tuple-element.36.near, bf16[256,4,128]{2,1,0:T(4,128)(2,1)} %copy-done.10, ...), custom_call_target="tpu_custom_call", output_to_operand_aliasing={{}: (5, {})} | custom-call | flops 4194304 | bytes 1572864 | tf_op jit(solution)/shard_map/unpack/pallas_call | solution.py:232
  164.7 5.4 %unpack.13.rest_0_ = bf16[2,4,32,16384]{3,2,1,0:T(8,128)(2,1)} custom-call(s32[2]{0:T(128)} %pad_add_fusion.where, s32[32]{0:T(128)} %reshape.235.lengths, s32[32]{0:T(128)} %reshape.236.offsets, bf16[256,4,128]{2,1,0:T(4,128)(2,1)} %copy-done.6, bf16[256,4,128]{2,1,0:T(4,128)(2,1)} %collective-permute-done.7.far, ...), custom_call_target="tpu_custom_call", output_to_operand_aliasing={{}: (5, {})} | custom-call | flops 4194304 | bytes 1572864 | tf_op jit(solution)/shard_map/unpack/pallas_call | solution.py:232
  171.5 5.4 %unpack.14.rest_0_ = bf16[2,4,32,16384]{3,2,1,0:T(8,128)(2,1)} custom-call(s32[2]{0:T(128)} %pad_add_fusion.where, s32[32]{0:T(128)} %reshape.235.lengths, s32[32]{0:T(128)} %reshape.236.offsets, bf16[256,4,128]{2,1,0:T(4,128)(2,1)} %copy-done.11, bf16[256,4,128]{2,1,0:T(4,128)(2,1)} %copy-done.12, ...), custom_call_target="tpu_custom_call", output_to_operand_aliasing={{}: (5, {})} | custom-call | flops 4194304 | bytes 1572864 | tf_op jit(solution)/shard_map/unpack/pallas_call | solution.py:232
  178.3 5.4 %unpack.15 = bf16[2,4,32,16384]{3,2,1,0:T(8,128)(2,1)} custom-call(s32[2]{0:T(128)} %pad_add_fusion.where, s32[32]{0:T(128)} %reshape.235.lengths, s32[32]{0:T(128)} %reshape.236.offsets, bf16[256,4,128]{2,1,0:T(4,128)(2,1)} %copy-done.8, bf16[256,4,128]{2,1,0:T(4,128)(2,1)} %copy-done.9, ...), custom_call_target="tpu_custom_call", output_to_operand_aliasing={{}: (5, {})} | custom-call | flops 4194304 | bytes 1572864 | tf_op jit(solution)/shard_map/unpack/pallas_call | solution.py:232
  (93 shorter events, 14.7 us)
Async XLA Ops:
  1.3 10.5 %collective-permute-start.1 = (f32[8,128]{1,0:T(8,128)S(1)}, f32[8,128]{1,0:T(8,128)S(1)}, u32[]{:S(2)}, u32[]{:S(2)}) collective-permute-start(f32[8,128]{1,0:T(8,128)S(1)} %bitcast.75), channel_id=1, source_target_pairs={{4,0},{8,4},{12,8},{16,12},{20,16},{24,20},{28,24},{5,1},{9,5},{13... | collective-permute-start | bytes 12296 | tf_op jit(solution)/shard_map/ppermute | solution.py:266
  2.6 9.3 %collective-permute-start = (f32[8,128]{1,0:T(8,128)S(1)}, f32[8,128]{1,0:T(8,128)S(1)}, u32[]{:S(2)}, u32[]{:S(2)}) collective-permute-start(f32[8,128]{1,0:T(8,128)S(1)} %bitcast.74), channel_id=1, source_target_pairs={{0,4},{4,8},{8,12},{12,16},{16,20},{20,24},{24,28},{1,5},{5,9},{9,... | collective-permute-start | bytes 12296 | tf_op jit(solution)/shard_map/ppermute | solution.py:266
  14.0 19.7 %copy-start.13 = (s32[8,32]{1,0:T(8,128)S(1)}, s32[8,32]{1,0:T(8,128)}, u32[]{:S(2)}) copy-start(s32[8,32]{1,0:T(8,128)} %owners.3) | copy-start | bytes 3076
  14.0 19.7 %copy-start.15 = (s32[8,32]{1,0:T(8,128)S(1)}, s32[8,32]{1,0:T(8,128)}, u32[]{:S(2)}) copy-start(s32[8,32]{1,0:T(8,128)} %lengths.3) | copy-start | bytes 3076
  29.8 80.2 %copy-start.14 = (s32[8,32]{1,0:T(8,128)S(1)}, s32[8,32]{1,0:T(8,128)}, u32[]{:S(2)}) copy-start(s32[8,32]{1,0:T(8,128)} %owners.3) | copy-start | bytes 3076
  29.8 90.4 %copy-start.16 = (s32[8,32]{1,0:T(8,128)S(1)}, s32[8,32]{1,0:T(8,128)}, u32[]{:S(2)}) copy-start(s32[8,32]{1,0:T(8,128)} %lengths.3) | copy-start | bytes 3076
  33.7 61.1 %copy-start.17 = (bf16[256,4,128]{2,1,0:T(4,128)(2,1)S(1)}, bf16[256,4,128]{2,1,0:T(4,128)(2,1)}, u32[]{:S(2)}) copy-start(bf16[256,4,128]{2,1,0:T(4,128)(2,1)} %get-tuple-element.34) | copy-start | bytes 786436
  50.8 11.8 %collective-permute-start.9 = (bf16[256,4,128]{2,1,0:T(4,128)(2,1)}, bf16[256,4,128]{2,1,0:T(4,128)(2,1)S(1)}, u32[]{:S(2)}, u32[]{:S(2)}) collective-permute-start(bf16[256,4,128]{2,1,0:T(4,128)(2,1)} %get-tuple-element.39), channel_id=1, source_target_pairs={{0,24},{4,28},{8,16},{12,20},{16,8},{20,12},{24,0},{28,4},{1,25},{... | collective-permute-start | bytes 786440 | tf_op jit(solution)/shard_map/ppermute | solution.py:287
  55.1 30.8 %collective-permute-start.10 = (bf16[256,4,128]{2,1,0:T(4,128)(2,1)}, bf16[256,4,128]{2,1,0:T(4,128)(2,1)S(1)}, u32[]{:S(2)}, u32[]{:S(2)}) collective-permute-start(bf16[256,4,128]{2,1,0:T(4,128)(2,1)} %get-tuple-element.40), channel_id=1, source_target_pairs={{0,28},{4,24},{8,20},{12,16},{16,12},{20,8},{24,4},{28,0},{1,29},{... | collective-permute-start | bytes 786440 | tf_op jit(solution)/shard_map/ppermute | solution.py:287
  57.0 37.8 %collective-permute-start.11 = (bf16[256,4,128]{2,1,0:T(4,128)(2,1)}, bf16[256,4,128]{2,1,0:T(4,128)(2,1)S(1)}, u32[]{:S(2)}, u32[]{:S(2)}) collective-permute-start(bf16[256,4,128]{2,1,0:T(4,128)(2,1)} %get-tuple-element.41), channel_id=1, source_target_pairs={{0,16},{4,20},{8,24},{12,28},{16,0},{20,4},{24,8},{28,12},{1,17},{... | collective-permute-start | bytes 786440 | tf_op jit(solution)/shard_map/ppermute | solution.py:287
  57.8 46.2 %collective-permute-start.12 = (bf16[256,4,128]{2,1,0:T(4,128)(2,1)}, bf16[256,4,128]{2,1,0:T(4,128)(2,1)S(1)}, u32[]{:S(2)}, u32[]{:S(2)}) collective-permute-start(bf16[256,4,128]{2,1,0:T(4,128)(2,1)} %get-tuple-element.42), channel_id=1, source_target_pairs={{0,20},{4,16},{8,28},{12,24},{16,4},{20,0},{24,12},{28,8},{1,21},{... | collective-permute-start | bytes 786440 | tf_op jit(solution)/shard_map/ppermute | solution.py:287
  59.0 51.0 %collective-permute-start.13 = (bf16[256,4,128]{2,1,0:T(4,128)(2,1)}, bf16[256,4,128]{2,1,0:T(4,128)(2,1)S(1)}, u32[]{:S(2)}, u32[]{:S(2)}) collective-permute-start(bf16[256,4,128]{2,1,0:T(4,128)(2,1)} %get-tuple-element.43), channel_id=1, source_target_pairs={{0,8},{4,12},{8,0},{12,4},{16,24},{20,28},{24,16},{28,20},{1,9},{5... | collective-permute-start | bytes 786440 | tf_op jit(solution)/shard_map/ppermute | solution.py:287
  62.6 85.9 %copy-start.1 = (bf16[256,4,128]{2,1,0:T(4,128)(2,1)}, bf16[256,4,128]{2,1,0:T(4,128)(2,1)S(1)}, u32[]{:S(2)}) copy-start(bf16[256,4,128]{2,1,0:T(4,128)(2,1)S(1)} %collective-permute-done.9.near) | copy-start | bytes 786436
  62.6 51.3 %collective-permute-start.14 = (bf16[256,4,128]{2,1,0:T(4,128)(2,1)}, bf16[256,4,128]{2,1,0:T(4,128)(2,1)S(1)}, u32[]{:S(2)}, u32[]{:S(2)}) collective-permute-start(bf16[256,4,128]{2,1,0:T(4,128)(2,1)} %get-tuple-element.44), channel_id=1, source_target_pairs={{0,12},{4,8},{8,4},{12,0},{16,28},{20,24},{24,20},{28,16},{1,13},{... | collective-permute-start | bytes 786440 | tf_op jit(solution)/shard_map/ppermute | solution.py:287
  85.8 68.1 %copy-start.2 = (bf16[256,4,128]{2,1,0:T(4,128)(2,1)}, bf16[256,4,128]{2,1,0:T(4,128)(2,1)S(1)}, u32[]{:S(2)}) copy-start(bf16[256,4,128]{2,1,0:T(4,128)(2,1)S(1)} %collective-permute-done.10.far) | copy-start | bytes 786436
  85.8 29.5 %collective-permute-start.15 = (bf16[256,4,128]{2,1,0:T(4,128)(2,1)}, bf16[256,4,128]{2,1,0:T(4,128)(2,1)S(1)}, u32[]{:S(2)}, u32[]{:S(2)}) collective-permute-start(bf16[256,4,128]{2,1,0:T(4,128)(2,1)} %get-tuple-element.46), channel_id=1, source_target_pairs={{0,4},{4,0},{8,12},{12,8},{16,20},{20,16},{24,28},{28,24},{1,5},{5... | collective-permute-start | bytes 786440 | tf_op jit(solution)/shard_map/ppermute | solution.py:287
  94.8 53.7 %copy-start.3 = (bf16[256,4,128]{2,1,0:T(4,128)(2,1)}, bf16[256,4,128]{2,1,0:T(4,128)(2,1)S(1)}, u32[]{:S(2)}) copy-start(bf16[256,4,128]{2,1,0:T(4,128)(2,1)S(1)} %collective-permute-done.11.near) | copy-start | bytes 786436
  94.8 21.1 %collective-permute-start.6 = (bf16[256,4,128]{2,1,0:T(4,128)(2,1)S(1)}, bf16[256,4,128]{2,1,0:T(4,128)(2,1)S(1)}, u32[]{:S(2)}, u32[]{:S(2)}) collective-permute-start(bf16[256,4,128]{2,1,0:T(4,128)(2,1)S(1)} %copy-done.17), channel_id=1, source_target_pairs={{0,8},{4,12},{8,0},{12,4},{16,24},{20,28},{24,16},{28,20},{1,9},{5... | collective-permute-start | bytes 786440 | tf_op jit(solution)/shard_map/ppermute | solution.py:287
  104.0 44.5 %copy-start.4 = (bf16[256,4,128]{2,1,0:T(4,128)(2,1)}, bf16[256,4,128]{2,1,0:T(4,128)(2,1)S(1)}, u32[]{:S(2)}) copy-start(bf16[256,4,128]{2,1,0:T(4,128)(2,1)S(1)} %collective-permute-done.12.far) | copy-start | bytes 786436
  104.0 13.8 %collective-permute-start.8 = (bf16[256,4,128]{2,1,0:T(4,128)(2,1)}, bf16[256,4,128]{2,1,0:T(4,128)(2,1)S(1)}, u32[]{:S(2)}, u32[]{:S(2)}) collective-permute-start(bf16[256,4,128]{2,1,0:T(4,128)(2,1)} %get-tuple-element.37), channel_id=1, source_target_pairs={{0,4},{4,0},{8,12},{12,8},{16,20},{20,16},{24,28},{28,24},{1,5},{5... | collective-permute-start | bytes 786440 | tf_op jit(solution)/shard_map/ppermute | solution.py:287
  104.8 32.2 %all-to-all-start = ((f32[6,4,32]{0,1,2:T(4,128)}), f32[6,4,32]{0,1,2:T(4,128)S(1)}, u32[]{:S(2)}, u32[]{:S(2)}) async-start(f32[6,4,32]{0,1,2:T(4,128)} %copy.66), calls=%async_computation | async-start | bytes 131072 | tf_op jit(solution)/shard_map/all_to_all | solution.py:322
  110.0 33.1 %copy-start.5 = (bf16[256,4,128]{2,1,0:T(4,128)(2,1)}, bf16[256,4,128]{2,1,0:T(4,128)(2,1)S(1)}, u32[]{:S(2)}) copy-start(bf16[256,4,128]{2,1,0:T(4,128)(2,1)S(1)} %collective-permute-done.13.near) | copy-start | bytes 786436
  110.0 66.9 %collective-permute-start.2 = (bf16[256,4,128]{2,1,0:T(4,128)(2,1)}, bf16[256,4,128]{2,1,0:T(4,128)(2,1)S(1)}, u32[]{:S(2)}, u32[]{:S(2)}) collective-permute-start(bf16[256,4,128]{2,1,0:T(4,128)(2,1)} %get-tuple-element.30), channel_id=1, source_target_pairs={{0,24},{4,28},{8,16},{12,20},{16,8},{20,12},{24,0},{28,4},{1,25},{... | collective-permute-start | bytes 786440 | tf_op jit(solution)/shard_map/ppermute | solution.py:287
  113.9 29.2 %copy-start.7 = (bf16[256,4,128]{2,1,0:T(4,128)(2,1)}, bf16[256,4,128]{2,1,0:T(4,128)(2,1)S(1)}, u32[]{:S(2)}) copy-start(bf16[256,4,128]{2,1,0:T(4,128)(2,1)S(1)} %collective-permute-done.14.far) | copy-start | bytes 786436
  113.9 63.1 %collective-permute-start.3 = (bf16[256,4,128]{2,1,0:T(4,128)(2,1)}, bf16[256,4,128]{2,1,0:T(4,128)(2,1)S(1)}, u32[]{:S(2)}, u32[]{:S(2)}) collective-permute-start(bf16[256,4,128]{2,1,0:T(4,128)(2,1)} %get-tuple-element.31), channel_id=1, source_target_pairs={{0,28},{4,24},{8,20},{12,16},{16,12},{20,8},{24,4},{28,0},{1,29},{... | collective-permute-start | bytes 786440 | tf_op jit(solution)/shard_map/ppermute | solution.py:287
  115.3 22.3 %copy-start = (bf16[256,4,128]{2,1,0:T(4,128)(2,1)}, bf16[256,4,128]{2,1,0:T(4,128)(2,1)S(1)}, u32[]{:S(2)}) copy-start(bf16[256,4,128]{2,1,0:T(4,128)(2,1)S(1)} %collective-permute-done.15.far) | copy-start | bytes 786436
  115.3 54.8 %collective-permute-start.4 = (bf16[256,4,128]{2,1,0:T(4,128)(2,1)}, bf16[256,4,128]{2,1,0:T(4,128)(2,1)S(1)}, u32[]{:S(2)}, u32[]{:S(2)}) collective-permute-start(bf16[256,4,128]{2,1,0:T(4,128)(2,1)} %get-tuple-element.32), channel_id=1, source_target_pairs={{0,16},{4,20},{8,24},{12,28},{16,0},{20,4},{24,8},{28,12},{1,17},{... | collective-permute-start | bytes 786440 | tf_op jit(solution)/shard_map/ppermute | solution.py:287
  115.9 32.6 %copy-start.6 = (bf16[256,4,128]{2,1,0:T(4,128)(2,1)}, bf16[256,4,128]{2,1,0:T(4,128)(2,1)S(1)}, u32[]{:S(2)}) copy-start(bf16[256,4,128]{2,1,0:T(4,128)(2,1)S(1)} %collective-permute-done.6.near) | copy-start | bytes 786436
  115.9 54.2 %collective-permute-start.5 = (bf16[256,4,128]{2,1,0:T(4,128)(2,1)}, bf16[256,4,128]{2,1,0:T(4,128)(2,1)S(1)}, u32[]{:S(2)}, u32[]{:S(2)}) collective-permute-start(bf16[256,4,128]{2,1,0:T(4,128)(2,1)} %get-tuple-element.33), channel_id=1, source_target_pairs={{0,20},{4,16},{8,28},{12,24},{16,4},{20,0},{24,12},{28,8},{1,21},{... | collective-permute-start | bytes 786440 | tf_op jit(solution)/shard_map/ppermute | solution.py:287
  117.8 30.7 %copy-start.10 = (bf16[256,4,128]{2,1,0:T(4,128)(2,1)}, bf16[256,4,128]{2,1,0:T(4,128)(2,1)S(1)}, u32[]{:S(2)}) copy-start(bf16[256,4,128]{2,1,0:T(4,128)(2,1)S(1)} %collective-permute-done.8.far) | copy-start | bytes 786436
  117.8 46.9 %collective-permute-start.7 = (bf16[256,4,128]{2,1,0:T(4,128)(2,1)}, bf16[256,4,128]{2,1,0:T(4,128)(2,1)}, u32[]{:S(2)}, u32[]{:S(2)}) collective-permute-start(bf16[256,4,128]{2,1,0:T(4,128)(2,1)} %get-tuple-element.35), channel_id=1, source_target_pairs={{0,12},{4,8},{8,4},{12,0},{16,28},{20,24},{24,20},{28,16},{1,13},{... | collective-permute-start | bytes 786440 | tf_op jit(solution)/shard_map/ppermute | solution.py:287
  170.2 0.7 copy-start.11
  (3 other events, 2.1 us)

commit v4 on v3

--- a/solution.py
+++ b/solution.py
@@ -189,43 +189,50 @@
 
 def unpack_kernel(chunk, pair, unit, where, lengths, offsets, near, far, *rest):
     out, work = rest[-2:]
-    m0 = pl.program_id(0) * chunk
     span, rows = near.shape[0], near.shape[1]
     slots = out.shape[2]
-    for half, got in enumerate((near, far)):
-        base_slot = (where[1] ^ half) * pair
-        for rank in range(pair):
-            j = (2 * unit + half) * pair + rank
-            n = lengths[j] - m0
-            base = offsets[j] + m0
-            lane = base_slot + rank
-
-            @pl.when(n >= chunk)
-            def _(got=got, base=base, lane=lane):
-                for m in range(chunk):
-                    work[m, pl.ds(lane, rows, stride=slots)] = got[base + m].astype(jnp.float32)
-
-            @pl.when(jnp.logical_and(n > 0, n < chunk))
-            def _(got=got, n=n, base=base, lane=lane):
-                for m in range(chunk):
-                    value = got[jnp.minimum(base + m, span - 1)].astype(jnp.float32)
-                    value = jnp.where(m < n, value, 0.0)
-                    work[m, pl.ds(lane, rows, stride=slots)] = value
-
-            @pl.when(n <= 0)
-            def _(lane=lane):
-                for m in range(chunk):
-                    work[m, pl.ds(lane, rows, stride=slots)] = jnp.zeros((rows, LANES), jnp.float32)
-
-    for m in range(chunk):
-        for r in range(rows):
-            out[0, r, :, m * LANES : (m + 1) * LANES] = work[m, r * slots : (r + 1) * slots].astype(jnp.bfloat16)
+    pieces = out.shape[3] // (chunk * LANES)
+
+    def one(piece, carry):
+        m0 = (pl.program_id(0) * pieces + piece) * chunk
+        for half, got in enumerate((near, far)):
+            base_slot = (where[1] ^ half) * pair
+            for rank in range(pair):
+                j = (2 * unit + half) * pair + rank
+                n = lengths[j] - m0
+                base = offsets[j] + m0
+                lane = base_slot + rank
+
+                @pl.when(n >= chunk)
+                def _(got=got, base=base, lane=lane):
+                    for m in range(chunk):
+                        work[m, pl.ds(lane, rows, stride=slots)] = got[base + m].astype(jnp.float32)
+
+                @pl.when(jnp.logical_and(n > 0, n < chunk))
+                def _(got=got, n=n, base=base, lane=lane):
+                    for m in range(chunk):
+                        value = got[jnp.minimum(base + m, span - 1)].astype(jnp.float32)
+                        value = jnp.where(m < n, value, 0.0)
+                        work[m, pl.ds(lane, rows, stride=slots)] = value
+
+                @pl.when(n <= 0)
+                def _(lane=lane):
+                    for m in range(chunk):
+                        work[m, pl.ds(lane, rows, stride=slots)] = jnp.zeros((rows, LANES), jnp.float32)
+
+        for m in range(chunk):
+            for r in range(rows):
+                out[0, r, :, pl.ds(pl.multiple_of((piece * chunk + m) * LANES, LANES), LANES)] = work[m, r * slots : (r + 1) * slots].astype(jnp.bfloat16)
+        return carry
+
+    lax.fori_loop(0, pieces, one, 0)
 
 
 def unpack(part, unit, where, lengths, offsets, near, far, dest, bins, pair, most):
     span, rows, _ = near.shape
     slots = 2 * pair
     chunk = min(16, most)
+    wide = min(64, most)
     whole = pl.BlockSpec((span, rows, LANES), lambda m, *_: (0, 0, 0))
     extra = [] if dest is None else [dest]
     size = rows * slots * most * LANES
@@ -233,15 +240,16 @@
         functools.partial(unpack_kernel, chunk, pair, unit),
         grid_spec=pltpu.PrefetchScalarGridSpec(
             num_scalar_prefetch=3,
-            grid=(most // chunk,),
+            grid=(most // wide,),
             in_specs=[whole, whole] + [pl.BlockSpec(memory_space=pl.ANY)] * len(extra),
             out_specs=pl.BlockSpec(
-                (1, rows, slots, chunk * LANES), lambda m, w, *_: (part, 0, w[0] ^ unit, m)
+                (1, rows, slots, wide * LANES), lambda m, w, *_: (part, 0, w[0] ^ unit, m)
             ),
             scratch_shapes=[pltpu.VMEM((chunk, rows * slots, LANES), jnp.float32)],
         ),
         out_shape=jax.ShapeDtypeStruct((2, rows, bins, most * LANES), jnp.bfloat16),
         input_output_aliases={5: 0} if extra else {},
+        compiler_params=pltpu.CompilerParams(vmem_limit_bytes=60 * 1024 * 1024),
         cost_estimate=pl.CostEstimate(flops=8 * size, bytes_accessed=3 * size, transcendentals=0),
         name="unpack",
     )(where, lengths, offsets, near, far, *extra)
@@ -287,7 +295,7 @@
             here[s] = lax.ppermute(packed[s], "freq", [(i, i ^ s) for i in range(n_freq)])
         got.append(here)
 
-    bin_blocks, bin_owner, got[1][0] = lax.optimization_barrier((bin_blocks, bin_owner, got[1][0]))
+    bin_blocks, bin_owner, got[0][0] = lax.optimization_barrier((bin_blocks, bin_owner, got[0][0]))
     position = jnp.arange(bins, dtype=jnp.int32)
     earlier = (position[None, :] < position[:, None])[None]
     same = bin_owner[:, :, None] == bin_owner[:, None, :]

time: 185 us -> 168 us (0.908)
  waiting for transfers between devices: 33.3 us -> 19.1 us
  Pallas kernels: 77.2 us -> 68.8 us
  starting transfers between devices: 55.5 us -> 61.2 us
    all_to_all x1, waiting for transfers between devices: 14.2 us -> 0.01 us  [local(): lax.all_to_all(local_summary, 'freq', split_axis=2, concat_axis=2, tiled=...]
    pallas_call x8, Pallas kernels: 43.2 us -> 34.8 us  [unpack(): pl.pallas_call(functools.partial(unpack_kernel, chunk, pair, unit), grid_...]
    all_to_all x1, starting transfers between devices: 5.2 us -> 9.05 us  [local(): lax.all_to_all(local_summary, 'freq', split_axis=2, concat_axis=2, tiled=...]
  transfers between devices with their start and end apart: 17 -> 17, of which waited for: 4 -> 2; matrix products, arithmetic and copies ran while one was open for 5% -> 5% of each run, Pallas kernels for 21% -> 18%
where the time goes in v4:
time: 168 us; the launch traced here: 167 us
  Pallas kernels  68.8 us (41%)
  starting transfers between devices  61.2 us (36%)
  waiting for transfers between devices  19.1 us (11%)
  local copies, waits for them, and re-layouts  10.9 us (6%)
  other arithmetic  6.04 us (4%)
    ppermute x14, starting transfers between devices, local(): lax.ppermute(packed[s], 'freq', [(i, i ^ s) for i in range(n_freq)])  45.3 us
    pallas_call x8, Pallas kernels, unpack(): pl.pallas_call(functools.partial(unpack_kernel, chunk, pair, unit), grid_...  34.8 us
    ppermute x14, waiting for transfers between devices, local(): lax.ppermute(packed[s], 'freq', [(i, i ^ s) for i in range(n_freq)])  19.1 us
    pallas_call x1, Pallas kernels, heterodyne(): pl.pallas_call(het_kernel, grid=(steps,), in_specs=[pl.BlockSpec((2, rows...  15.8 us
    pallas_call x1, Pallas kernels, bin_sums(): pl.pallas_call(functools.partial(sums_kernel, tmpl_rows), grid=(total //...  10.5 us
    all_to_all x1, starting transfers between devices, local(): lax.all_to_all(local_summary, 'freq', split_axis=2, concat_axis=2, tiled=...  9.05 us
    pallas_call x2, Pallas kernels, pack(): pl.pallas_call(pack_kernel, grid_spec=pltpu.PrefetchScalarGridSpec(num_sc...  7.7 us
    ppermute x1, starting transfers between devices, local(): lax.ppermute(psd_v[-8:], 'freq', up)  5.5 us
  transfers between devices with their start and end apart: 17, of which 2 were waited for; matrix products, arithmetic and copies ran while one was open for 5% of the time, Pallas kernels for 18%

profile of v4, /device:TPU:0, one launch (start us, length us, event | category | flops | bytes accessed | tf_op | source)
XLA Modules:
  0.0 167.0 jit_solution(7508939314447948414)
XLA Ops:
  1.3 1.3 collective-permute-start.1
  2.6 5.5 %collective-permute-start = (f32[8,128]{1,0:T(8,128)S(1)}, f32[8,128]{1,0:T(8,128)S(1)}, u32[]{:S(2)}, u32[]{:S(2)}) collective-permute-start(f32[8,128]{1,0:T(8,128)S(1)} %bitcast.74), channel_id=1, source_target_pairs={{0,4},{4,8},{8,12},{12,16},{16,20},{20,24},{24,28},{1,5},{5,9},{9,... | collective-permute-start | bytes 12296 | tf_op jit(solution)/shard_map/ppermute | solution.py:274
  9.1 0.8 fusion.10
  9.9 1.3 multiply_sine_fusion
  13.3 0.8 broadcast_in_dim.102.cos_s
  14.1 15.8 %heterodyne.1 = (bf16[8192,128]{1,0:T(8,128)(2,1)}, bf16[8192,128]{1,0:T(8,128)(2,1)}, bf16[8192,128]{1,0:T(8,128)(2,1)}) custom-call(bf16[2,8192,128]{2,1,0:T(8,128)(2,1)} %bitcast.68, bf16[2,8192,128]{2,1,0:T(8,128)(2,1)} %bitcast.69, f32[8192,128]{1,0:T(8,128)} %bitcast.63, f32[8192,128]{1,0:T(8,128)} %bitcast.64, f32[8192,128]{1,0:T(8,128)} %bitcast.65, ...), custom_call_target="tpu_custom_call" | custom-call | flops 62914560 | bytes 18874368 | tf_op jit(solution)/shard_map/heterodyne/pallas_call | solution.py:62
  29.9 4.0 %pack.2 = (bf16[256,4,128]{2,1,0:T(4,128)(2,1)}, bf16[256,4,128]{2,1,0:T(4,128)(2,1)}, bf16[256,4,128]{2,1,0:T(4,128)(2,1)}, bf16[256,4,128]{2,1,0:T(4,128)(2,1)...) custom-call(s32[8,32]{1,0:T(8,128)} %lengths.3, ...), custom_call_target="tpu_custom_call" | custom-call | bytes 4194304 | tf_op jit(solution)/shard_map/pack/pallas_call | solution.py:174
  35.9 10.5 %sums.1 = (f32[8,128]{1,0:T(8,128)}, f32[8,128]{1,0:T(8,128)}) custom-call(bf16[8192,128]{1,0:T(8,128)(2,1)} %get-tuple-element.26.real, bf16[8192,128]{1,0:T(8,128)(2,1)} %get-tuple-element.30.imag, bf16[8192,128]{1,0:T(8,128)(2,1)} %get-tuple-element.47.power, s32[1,128]{1,0:T(1,128)} %broadcast_in_dim_tile.8.first, s32[1,128]{1,0:T(1,128)} %broadcast_in_dim_tile.9.length), custom_call_target="tpu_custom_call" | custom-call | flops 209715200 | bytes 6291456 | tf_op jit(solution)/shard_map/sums/pallas_call | solution.py:121
  46.4 0.8 reshape.238
  47.2 3.7 %pack.3 = (bf16[256,4,128]{2,1,0:T(4,128)(2,1)}, bf16[256,4,128]{2,1,0:T(4,128)(2,1)}, bf16[256,4,128]{2,1,0:T(4,128)(2,1)}, bf16[256,4,128]{2,1,0:T(4,128)(2,1)...) custom-call(s32[8,32]{1,0:T(8,128)} %lengths.3, ...), custom_call_target="tpu_custom_call" | custom-call | bytes 4194304 | tf_op jit(solution)/shard_map/pack/pallas_call | solution.py:174
  50.9 2.2 %collective-permute-start.6 = (bf16[256,4,128]{2,1,0:T(4,128)(2,1)}, bf16[256,4,128]{2,1,0:T(4,128)(2,1)S(1)}, u32[]{:S(2)}, u32[]{:S(2)}) collective-permute-start(bf16[256,4,128]{2,1,0:T(4,128)(2,1)} %get-tuple-element.35), channel_id=1, source_target_pairs={{0,8},{4,12},{8,0},{12,4},{16,24},{20,28},{24,16},{28,20},{1,9},{5... | collective-permute-start | bytes 786440 | tf_op jit(solution)/shard_map/ppermute | solution.py:295
  53.1 2.4 %collective-permute-start.8 = (bf16[256,4,128]{2,1,0:T(4,128)(2,1)}, bf16[256,4,128]{2,1,0:T(4,128)(2,1)S(1)}, u32[]{:S(2)}, u32[]{:S(2)}) collective-permute-start(bf16[256,4,128]{2,1,0:T(4,128)(2,1)} %get-tuple-element.38), channel_id=1, source_target_pairs={{0,4},{4,0},{8,12},{12,8},{16,20},{20,16},{24,28},{28,24},{1,5},{5... | collective-permute-start | bytes 786440 | tf_op jit(solution)/shard_map/ppermute | solution.py:295
  56.3 2.5 %collective-permute-start.9 = (bf16[256,4,128]{2,1,0:T(4,128)(2,1)S(1)}, bf16[256,4,128]{2,1,0:T(4,128)(2,1)S(1)}, u32[]{:S(2)}, u32[]{:S(2)}) collective-permute-start(bf16[256,4,128]{2,1,0:T(4,128)(2,1)S(1)} %copy-done.21), channel_id=1, source_target_pairs={{0,24},{4,28},{8,16},{12,20},{16,8},{20,12},{24,0},{28,4},{1,25},{... | collective-permute-start | bytes 786440 | tf_op jit(solution)/shard_map/ppermute | solution.py:295
  58.8 0.8 collective-permute-start.10
  60.0 5.3 %collective-permute-start.12 = (bf16[256,4,128]{2,1,0:T(4,128)(2,1)S(1)}, bf16[256,4,128]{2,1,0:T(4,128)(2,1)S(1)}, u32[]{:S(2)}, u32[]{:S(2)}) collective-permute-start(bf16[256,4,128]{2,1,0:T(4,128)(2,1)S(1)} %copy-done.19), channel_id=1, source_target_pairs={{0,20},{4,16},{8,28},{12,24},{16,4},{20,0},{24,12},{28,8},{1,21},{... | collective-permute-start | bytes 786440 | tf_op jit(solution)/shard_map/ppermute | solution.py:295
  65.4 3.3 %collective-permute-done.9.near = bf16[256,4,128]{2,1,0:T(4,128)(2,1)S(1)} collective-permute-done((bf16[256,4,128]{2,1,0:T(4,128)(2,1)S(1)}, bf16[256,4,128]{2,1,0:T(4,128)(2,1)S(1)}, u32[]{:S(2)}, u32[]{:S(2)}) %collective-permute-start.9) | collective-permute-done | bytes 262176 | tf_op jit(solution)/shard_map/ppermute | solution.py:295
  68.8 19.4 %collective-permute-start.14 = (bf16[256,4,128]{2,1,0:T(4,128)(2,1)S(1)}, bf16[256,4,128]{2,1,0:T(4,128)(2,1)S(1)}, u32[]{:S(2)}, u32[]{:S(2)}) collective-permute-start(bf16[256,4,128]{2,1,0:T(4,128)(2,1)S(1)} %copy-done.17), channel_id=1, source_target_pairs={{0,12},{4,8},{8,4},{12,0},{16,28},{20,24},{24,20},{28,16},{1,13},{... | collective-permute-start | bytes 786440 | tf_op jit(solution)/shard_map/ppermute | solution.py:295
  88.2 1.6 collective-permute-start.15
  90.5 9.1 %all-to-all-start = ((f32[6,4,32]{0,1,2:T(4,128)}), f32[6,4,32]{0,1,2:T(4,128)S(1)}, u32[]{:S(2)}, u32[]{:S(2)}) async-start(f32[6,4,32]{0,1,2:T(4,128)} %copy.66), calls=%async_computation | async-start | bytes 131072 | tf_op jit(solution)/shard_map/all_to_all | solution.py:330
  99.6 3.9 %collective-permute-start.2 = (bf16[256,4,128]{2,1,0:T(4,128)(2,1)}, bf16[256,4,128]{2,1,0:T(4,128)(2,1)S(1)}, u32[]{:S(2)}, u32[]{:S(2)}) collective-permute-start(bf16[256,4,128]{2,1,0:T(4,128)(2,1)} %get-tuple-element.31), channel_id=1, source_target_pairs={{0,24},{4,28},{8,16},{12,20},{16,8},{20,12},{24,0},{28,4},{1,25},{... | collective-permute-start | bytes 786440 | tf_op jit(solution)/shard_map/ppermute | solution.py:295
  103.5 15.8 %collective-permute-done.12.far = bf16[256,4,128]{2,1,0:T(4,128)(2,1)S(1)} collective-permute-done((bf16[256,4,128]{2,1,0:T(4,128)(2,1)S(1)}, bf16[256,4,128]{2,1,0:T(4,128)(2,1)S(1)}, u32[]{:S(2)}, u32[]{:S(2)}) %collective-permute-start.12) | collective-permute-done | bytes 262176 | tf_op jit(solution)/shard_map/ppermute | solution.py:295
  119.3 3.6 %collective-permute-start.3 = (bf16[256,4,128]{2,1,0:T(4,128)(2,1)}, bf16[256,4,128]{2,1,0:T(4,128)(2,1)S(1)}, u32[]{:S(2)}, u32[]{:S(2)}) collective-permute-start(bf16[256,4,128]{2,1,0:T(4,128)(2,1)} %get-tuple-element.32), channel_id=1, source_target_pairs={{0,28},{4,24},{8,20},{12,16},{16,12},{20,8},{24,4},{28,0},{1,29},{... | collective-permute-start | bytes 786440 | tf_op jit(solution)/shard_map/ppermute | solution.py:295
  122.8 3.2 %collective-permute-start.5 = (bf16[256,4,128]{2,1,0:T(4,128)(2,1)}, bf16[256,4,128]{2,1,0:T(4,128)(2,1)S(1)}, u32[]{:S(2)}, u32[]{:S(2)}) collective-permute-start(bf16[256,4,128]{2,1,0:T(4,128)(2,1)} %get-tuple-element.34), channel_id=1, source_target_pairs={{0,20},{4,16},{8,28},{12,24},{16,4},{20,0},{24,12},{28,8},{1,21},{... | collective-permute-start | bytes 786440 | tf_op jit(solution)/shard_map/ppermute | solution.py:295
  126.1 1.3 fusion.1
  129.3 4.4 %unpack.8.rest_0_ = bf16[2,4,32,16384]{3,2,1,0:T(8,128)(2,1)} custom-call(s32[2]{0:T(128)} %pad_add_fusion.where, s32[32]{0:T(128)} %reshape.235.lengths, s32[32]{0:T(128)} %reshape.236.offsets, bf16[256,4,128]{2,1,0:T(4,128)(2,1)} %get-tuple-element.45.near, bf16[256,4,128]{2,1,0:T(4,128)(2,1)} %copy-done), custom_call_target="tpu_custom_call" | custom-call | flops 4194304 | bytes 1572864 | tf_op jit(solution)/shard_map/unpack/pallas_call | solution.py:239
  133.7 4.4 %unpack.9.rest_0_ = bf16[2,4,32,16384]{3,2,1,0:T(8,128)(2,1)} custom-call(s32[2]{0:T(128)} %pad_add_fusion.where, s32[32]{0:T(128)} %reshape.235.lengths, s32[32]{0:T(128)} %reshape.236.offsets, bf16[256,4,128]{2,1,0:T(4,128)(2,1)} %copy-done.8, bf16[256,4,128]{2,1,0:T(4,128)(2,1)} %copy-done.10, ...), custom_call_target="tpu_custom_call", output_to_operand_aliasing={{}: (5, {})} | custom-call | flops 4194304 | bytes 1572864 | tf_op jit(solution)/shard_map/unpack/pallas_call | solution.py:239
  138.1 4.3 %unpack.10.rest_0_ = bf16[2,4,32,16384]{3,2,1,0:T(8,128)(2,1)} custom-call(s32[2]{0:T(128)} %pad_add_fusion.where, s32[32]{0:T(128)} %reshape.235.lengths, s32[32]{0:T(128)} %reshape.236.offsets, bf16[256,4,128]{2,1,0:T(4,128)(2,1)} %copy-done.5, bf16[256,4,128]{2,1,0:T(4,128)(2,1)} %copy-done.6, ...), custom_call_target="tpu_custom_call", output_to_operand_aliasing={{}: (5, {})} | custom-call | flops 4194304 | bytes 1572864 | tf_op jit(solution)/shard_map/unpack/pallas_call | solution.py:239
  142.4 4.4 %unpack.11.rest_0_ = bf16[2,4,32,16384]{3,2,1,0:T(8,128)(2,1)} custom-call(s32[2]{0:T(128)} %pad_add_fusion.where, s32[32]{0:T(128)} %reshape.235.lengths, s32[32]{0:T(128)} %reshape.236.offsets, bf16[256,4,128]{2,1,0:T(4,128)(2,1)} %copy-done.3, bf16[256,4,128]{2,1,0:T(4,128)(2,1)} %copy-done.4, ...), custom_call_target="tpu_custom_call", output_to_operand_aliasing={{}: (5, {})} | custom-call | flops 4194304 | bytes 1572864 | tf_op jit(solution)/shard_map/unpack/pallas_call | solution.py:239
  146.7 4.4 %unpack.12.rest_0_ = bf16[2,4,32,16384]{3,2,1,0:T(8,128)(2,1)} custom-call(s32[2]{0:T(128)} %pad_add_fusion.where, s32[32]{0:T(128)} %reshape.235.lengths, s32[32]{0:T(128)} %reshape.236.offsets, bf16[256,4,128]{2,1,0:T(4,128)(2,1)} %get-tuple-element.37.near, bf16[256,4,128]{2,1,0:T(4,128)(2,1)} %copy-done.2, ...), custom_call_target="tpu_custom_call", output_to_operand_aliasing={{}: (5, {})} | custom-call | flops 4194304 | bytes 1572864 | tf_op jit(solution)/shard_map/unpack/pallas_call | solution.py:239
  151.1 4.4 %unpack.13.rest_0_ = bf16[2,4,32,16384]{3,2,1,0:T(8,128)(2,1)} custom-call(s32[2]{0:T(128)} %pad_add_fusion.where, s32[32]{0:T(128)} %reshape.235.lengths, s32[32]{0:T(128)} %reshape.236.offsets, bf16[256,4,128]{2,1,0:T(4,128)(2,1)} %copy-done.1, bf16[256,4,128]{2,1,0:T(4,128)(2,1)} %collective-permute-done.7.far, ...), custom_call_target="tpu_custom_call", output_to_operand_aliasing={{}: (5, {})} | custom-call | flops 4194304 | bytes 1572864 | tf_op jit(solution)/shard_map/unpack/pallas_call | solution.py:239
  156.9 4.3 %unpack.14.rest_0_ = bf16[2,4,32,16384]{3,2,1,0:T(8,128)(2,1)} custom-call(s32[2]{0:T(128)} %pad_add_fusion.where, s32[32]{0:T(128)} %reshape.235.lengths, s32[32]{0:T(128)} %reshape.236.offsets, bf16[256,4,128]{2,1,0:T(4,128)(2,1)} %copy-done.11, bf16[256,4,128]{2,1,0:T(4,128)(2,1)} %copy-done.12, ...), custom_call_target="tpu_custom_call", output_to_operand_aliasing={{}: (5, {})} | custom-call | flops 4194304 | bytes 1572864 | tf_op jit(solution)/shard_map/unpack/pallas_call | solution.py:239
  162.6 4.4 %unpack.15 = bf16[2,4,32,16384]{3,2,1,0:T(8,128)(2,1)} custom-call(s32[2]{0:T(128)} %pad_add_fusion.where, s32[32]{0:T(128)} %reshape.235.lengths, s32[32]{0:T(128)} %reshape.236.offsets, bf16[256,4,128]{2,1,0:T(4,128)(2,1)} %copy-done.7, bf16[256,4,128]{2,1,0:T(4,128)(2,1)} %copy-done.9, ...), custom_call_target="tpu_custom_call", output_to_operand_aliasing={{}: (5, {})} | custom-call | flops 4194304 | bytes 1572864 | tf_op jit(solution)/shard_map/unpack/pallas_call | solution.py:239
  (101 shorter events, 12.6 us)
Async XLA Ops:
  1.3 10.6 %collective-permute-start.1 = (f32[8,128]{1,0:T(8,128)S(1)}, f32[8,128]{1,0:T(8,128)S(1)}, u32[]{:S(2)}, u32[]{:S(2)}) collective-permute-start(f32[8,128]{1,0:T(8,128)S(1)} %bitcast.75), channel_id=1, source_target_pairs={{4,0},{8,4},{12,8},{16,12},{20,16},{24,20},{28,24},{5,1},{9,5},{13... | collective-permute-start | bytes 12296 | tf_op jit(solution)/shard_map/ppermute | solution.py:274
  2.6 9.3 %collective-permute-start = (f32[8,128]{1,0:T(8,128)S(1)}, f32[8,128]{1,0:T(8,128)S(1)}, u32[]{:S(2)}, u32[]{:S(2)}) collective-permute-start(f32[8,128]{1,0:T(8,128)S(1)} %bitcast.74), channel_id=1, source_target_pairs={{0,4},{4,8},{8,12},{12,16},{16,20},{20,24},{24,28},{1,5},{5,9},{9,... | collective-permute-start | bytes 12296 | tf_op jit(solution)/shard_map/ppermute | solution.py:274
  14.1 19.8 %copy-start.13 = (s32[8,32]{1,0:T(8,128)S(1)}, s32[8,32]{1,0:T(8,128)}, u32[]{:S(2)}) copy-start(s32[8,32]{1,0:T(8,128)} %owners.3) | copy-start | bytes 3076
  14.1 19.9 %copy-start.15 = (s32[8,32]{1,0:T(8,128)S(1)}, s32[8,32]{1,0:T(8,128)}, u32[]{:S(2)}) copy-start(s32[8,32]{1,0:T(8,128)} %lengths.3) | copy-start | bytes 3076
  29.9 69.7 %copy-start.14 = (s32[8,32]{1,0:T(8,128)S(1)}, s32[8,32]{1,0:T(8,128)}, u32[]{:S(2)}) copy-start(s32[8,32]{1,0:T(8,128)} %owners.3) | copy-start | bytes 3076
  29.9 96.1 %copy-start.16 = (s32[8,32]{1,0:T(8,128)S(1)}, s32[8,32]{1,0:T(8,128)}, u32[]{:S(2)}) copy-start(s32[8,32]{1,0:T(8,128)} %lengths.3) | copy-start | bytes 3076
  33.9 22.4 %copy-start.21 = (bf16[256,4,128]{2,1,0:T(4,128)(2,1)S(1)}, bf16[256,4,128]{2,1,0:T(4,128)(2,1)}, u32[]{:S(2)}) copy-start(bf16[256,4,128]{2,1,0:T(4,128)(2,1)} %get-tuple-element.39) | copy-start | bytes 786436
  33.9 24.9 %copy-start.20 = (bf16[256,4,128]{2,1,0:T(4,128)(2,1)S(1)}, bf16[256,4,128]{2,1,0:T(4,128)(2,1)}, u32[]{:S(2)}) copy-start(bf16[256,4,128]{2,1,0:T(4,128)(2,1)} %get-tuple-element.40) | copy-start | bytes 786436
  33.9 26.1 %copy-start.19 = (bf16[256,4,128]{2,1,0:T(4,128)(2,1)S(1)}, bf16[256,4,128]{2,1,0:T(4,128)(2,1)}, u32[]{:S(2)}) copy-start(bf16[256,4,128]{2,1,0:T(4,128)(2,1)} %get-tuple-element.42) | copy-start | bytes 786436
  33.9 31.4 %copy-start.18 = (bf16[256,4,128]{2,1,0:T(4,128)(2,1)S(1)}, bf16[256,4,128]{2,1,0:T(4,128)(2,1)}, u32[]{:S(2)}) copy-start(bf16[256,4,128]{2,1,0:T(4,128)(2,1)} %get-tuple-element.43) | copy-start | bytes 786436
  33.9 34.8 %copy-start.17 = (bf16[256,4,128]{2,1,0:T(4,128)(2,1)S(1)}, bf16[256,4,128]{2,1,0:T(4,128)(2,1)}, u32[]{:S(2)}) copy-start(bf16[256,4,128]{2,1,0:T(4,128)(2,1)} %get-tuple-element.44) | copy-start | bytes 786436
  50.9 9.1 %collective-permute-start.6 = (bf16[256,4,128]{2,1,0:T(4,128)(2,1)}, bf16[256,4,128]{2,1,0:T(4,128)(2,1)S(1)}, u32[]{:S(2)}, u32[]{:S(2)}) collective-permute-start(bf16[256,4,128]{2,1,0:T(4,128)(2,1)} %get-tuple-element.35), channel_id=1, source_target_pairs={{0,8},{4,12},{8,0},{12,4},{16,24},{20,28},{24,16},{28,20},{1,9},{5... | collective-permute-start | bytes 786440 | tf_op jit(solution)/shard_map/ppermute | solution.py:295
  53.1 12.2 %collective-permute-start.8 = (bf16[256,4,128]{2,1,0:T(4,128)(2,1)}, bf16[256,4,128]{2,1,0:T(4,128)(2,1)S(1)}, u32[]{:S(2)}, u32[]{:S(2)}) collective-permute-start(bf16[256,4,128]{2,1,0:T(4,128)(2,1)} %get-tuple-element.38), channel_id=1, source_target_pairs={{0,4},{4,0},{8,12},{12,8},{16,20},{20,16},{24,28},{28,24},{1,5},{5... | collective-permute-start | bytes 786440 | tf_op jit(solution)/shard_map/ppermute | solution.py:295
  56.3 12.5 %collective-permute-start.9 = (bf16[256,4,128]{2,1,0:T(4,128)(2,1)S(1)}, bf16[256,4,128]{2,1,0:T(4,128)(2,1)S(1)}, u32[]{:S(2)}, u32[]{:S(2)}) collective-permute-start(bf16[256,4,128]{2,1,0:T(4,128)(2,1)S(1)} %copy-done.21), channel_id=1, source_target_pairs={{0,24},{4,28},{8,16},{12,20},{16,8},{20,12},{24,0},{28,4},{1,25},{... | collective-permute-start | bytes 786440 | tf_op jit(solution)/shard_map/ppermute | solution.py:295
  58.8 29.4 %collective-permute-start.10 = (bf16[256,4,128]{2,1,0:T(4,128)(2,1)S(1)}, bf16[256,4,128]{2,1,0:T(4,128)(2,1)S(1)}, u32[]{:S(2)}, u32[]{:S(2)}) collective-permute-start(bf16[256,4,128]{2,1,0:T(4,128)(2,1)S(1)} %copy-done.20), channel_id=1, source_target_pairs={{0,28},{4,24},{8,20},{12,16},{16,12},{20,8},{24,4},{28,0},{1,29},{... | collective-permute-start | bytes 786440 | tf_op jit(solution)/shard_map/ppermute | solution.py:295
  59.6 40.0 %collective-permute-start.11 = (bf16[256,4,128]{2,1,0:T(4,128)(2,1)}, bf16[256,4,128]{2,1,0:T(4,128)(2,1)S(1)}, u32[]{:S(2)}, u32[]{:S(2)}) collective-permute-start(bf16[256,4,128]{2,1,0:T(4,128)(2,1)} %get-tuple-element.41), channel_id=1, source_target_pairs={{0,16},{4,20},{8,24},{12,28},{16,0},{20,4},{24,8},{28,12},{1,17},{... | collective-permute-start | bytes 786440 | tf_op jit(solution)/shard_map/ppermute | solution.py:295
  60.0 78.0 %copy-start.1 = (bf16[256,4,128]{2,1,0:T(4,128)(2,1)}, bf16[256,4,128]{2,1,0:T(4,128)(2,1)S(1)}, u32[]{:S(2)}) copy-start(bf16[256,4,128]{2,1,0:T(4,128)(2,1)S(1)} %collective-permute-done.6.near) | copy-start | bytes 786436
  60.0 59.2 %collective-permute-start.12 = (bf16[256,4,128]{2,1,0:T(4,128)(2,1)S(1)}, bf16[256,4,128]{2,1,0:T(4,128)(2,1)S(1)}, u32[]{:S(2)}, u32[]{:S(2)}) collective-permute-start(bf16[256,4,128]{2,1,0:T(4,128)(2,1)S(1)} %copy-done.19), channel_id=1, source_target_pairs={{0,20},{4,16},{8,28},{12,24},{16,4},{20,0},{24,12},{28,8},{1,21},{... | collective-permute-start | bytes 786440 | tf_op jit(solution)/shard_map/ppermute | solution.py:295
  65.4 81.4 %copy-start.2 = (bf16[256,4,128]{2,1,0:T(4,128)(2,1)}, bf16[256,4,128]{2,1,0:T(4,128)(2,1)S(1)}, u32[]{:S(2)}) copy-start(bf16[256,4,128]{2,1,0:T(4,128)(2,1)S(1)} %collective-permute-done.8.far) | copy-start | bytes 786436
  65.4 57.5 %collective-permute-start.13 = (bf16[256,4,128]{2,1,0:T(4,128)(2,1)S(1)}, bf16[256,4,128]{2,1,0:T(4,128)(2,1)S(1)}, u32[]{:S(2)}, u32[]{:S(2)}) collective-permute-start(bf16[256,4,128]{2,1,0:T(4,128)(2,1)S(1)} %copy-done.18), channel_id=1, source_target_pairs={{0,8},{4,12},{8,0},{12,4},{16,24},{20,28},{24,16},{28,20},{1,9},{5... | collective-permute-start | bytes 786440 | tf_op jit(solution)/shard_map/ppermute | solution.py:295
  68.7 73.6 %copy-start.3 = (bf16[256,4,128]{2,1,0:T(4,128)(2,1)}, bf16[256,4,128]{2,1,0:T(4,128)(2,1)S(1)}, u32[]{:S(2)}) copy-start(bf16[256,4,128]{2,1,0:T(4,128)(2,1)S(1)} %collective-permute-done.9.near) | copy-start | bytes 786436
  68.8 54.1 %collective-permute-start.14 = (bf16[256,4,128]{2,1,0:T(4,128)(2,1)S(1)}, bf16[256,4,128]{2,1,0:T(4,128)(2,1)S(1)}, u32[]{:S(2)}, u32[]{:S(2)}) collective-permute-start(bf16[256,4,128]{2,1,0:T(4,128)(2,1)S(1)} %copy-done.17), channel_id=1, source_target_pairs={{0,12},{4,8},{8,4},{12,0},{16,28},{20,24},{24,20},{28,16},{1,13},{... | collective-permute-start | bytes 786440 | tf_op jit(solution)/shard_map/ppermute | solution.py:295
  88.2 54.2 %copy-start.4 = (bf16[256,4,128]{2,1,0:T(4,128)(2,1)}, bf16[256,4,128]{2,1,0:T(4,128)(2,1)S(1)}, u32[]{:S(2)}) copy-start(bf16[256,4,128]{2,1,0:T(4,128)(2,1)S(1)} %collective-permute-done.10.far) | copy-start | bytes 786436
  88.2 37.8 %collective-permute-start.15 = (bf16[256,4,128]{2,1,0:T(4,128)(2,1)}, bf16[256,4,128]{2,1,0:T(4,128)(2,1)S(1)}, u32[]{:S(2)}, u32[]{:S(2)}) collective-permute-start(bf16[256,4,128]{2,1,0:T(4,128)(2,1)} %get-tuple-element.46), channel_id=1, source_target_pairs={{0,4},{4,0},{8,12},{12,8},{16,20},{20,16},{24,28},{28,24},{1,5},{5... | collective-permute-start | bytes 786440 | tf_op jit(solution)/shard_map/ppermute | solution.py:295
  90.5 38.1 %all-to-all-start = ((f32[6,4,32]{0,1,2:T(4,128)}), f32[6,4,32]{0,1,2:T(4,128)S(1)}, u32[]{:S(2)}, u32[]{:S(2)}) async-start(f32[6,4,32]{0,1,2:T(4,128)} %copy.66), calls=%async_computation | async-start | bytes 131072 | tf_op jit(solution)/shard_map/all_to_all | solution.py:330
  99.6 38.5 %copy-start.5 = (bf16[256,4,128]{2,1,0:T(4,128)(2,1)}, bf16[256,4,128]{2,1,0:T(4,128)(2,1)S(1)}, u32[]{:S(2)}) copy-start(bf16[256,4,128]{2,1,0:T(4,128)(2,1)S(1)} %collective-permute-done.11.near) | copy-start | bytes 786436
  99.6 61.6 %collective-permute-start.2 = (bf16[256,4,128]{2,1,0:T(4,128)(2,1)}, bf16[256,4,128]{2,1,0:T(4,128)(2,1)S(1)}, u32[]{:S(2)}, u32[]{:S(2)}) collective-permute-start(bf16[256,4,128]{2,1,0:T(4,128)(2,1)} %get-tuple-element.31), channel_id=1, source_target_pairs={{0,24},{4,28},{8,16},{12,20},{16,8},{20,12},{24,0},{28,4},{1,25},{... | collective-permute-start | bytes 786440 | tf_op jit(solution)/shard_map/ppermute | solution.py:295
  119.3 18.8 %copy-start.6 = (bf16[256,4,128]{2,1,0:T(4,128)(2,1)}, bf16[256,4,128]{2,1,0:T(4,128)(2,1)S(1)}, u32[]{:S(2)}) copy-start(bf16[256,4,128]{2,1,0:T(4,128)(2,1)S(1)} %collective-permute-done.12.far) | copy-start | bytes 786436
  119.3 42.0 %collective-permute-start.3 = (bf16[256,4,128]{2,1,0:T(4,128)(2,1)}, bf16[256,4,128]{2,1,0:T(4,128)(2,1)S(1)}, u32[]{:S(2)}, u32[]{:S(2)}) collective-permute-start(bf16[256,4,128]{2,1,0:T(4,128)(2,1)} %get-tuple-element.32), channel_id=1, source_target_pairs={{0,28},{4,24},{8,20},{12,16},{16,12},{20,8},{24,4},{28,0},{1,29},{... | collective-permute-start | bytes 786440 | tf_op jit(solution)/shard_map/ppermute | solution.py:295
  122.8 32.7 %collective-permute-start.4 = (bf16[256,4,128]{2,1,0:T(4,128)(2,1)}, bf16[256,4,128]{2,1,0:T(4,128)(2,1)S(1)}, u32[]{:S(2)}, u32[]{:S(2)}) collective-permute-start(bf16[256,4,128]{2,1,0:T(4,128)(2,1)} %get-tuple-element.33), channel_id=1, source_target_pairs={{0,16},{4,20},{8,24},{12,28},{16,0},{20,4},{24,8},{28,12},{1,17},{... | collective-permute-start | bytes 786440 | tf_op jit(solution)/shard_map/ppermute | solution.py:295
  122.8 32.6 %collective-permute-start.5 = (bf16[256,4,128]{2,1,0:T(4,128)(2,1)}, bf16[256,4,128]{2,1,0:T(4,128)(2,1)S(1)}, u32[]{:S(2)}, u32[]{:S(2)}) collective-permute-start(bf16[256,4,128]{2,1,0:T(4,128)(2,1)} %get-tuple-element.34), channel_id=1, source_target_pairs={{0,20},{4,16},{8,28},{12,24},{16,4},{20,0},{24,12},{28,8},{1,21},{... | collective-permute-start | bytes 786440 | tf_op jit(solution)/shard_map/ppermute | solution.py:295
  126.0 25.1 %collective-permute-start.7 = (bf16[256,4,128]{2,1,0:T(4,128)(2,1)}, bf16[256,4,128]{2,1,0:T(4,128)(2,1)}, u32[]{:S(2)}, u32[]{:S(2)}) collective-permute-start(bf16[256,4,128]{2,1,0:T(4,128)(2,1)} %get-tuple-element.36), channel_id=1, source_target_pairs={{0,12},{4,8},{8,4},{12,0},{16,28},{20,24},{24,20},{28,16},{1,13},{... | collective-permute-start | bytes 786440 | tf_op jit(solution)/shard_map/ppermute | solution.py:295
  (7 other events, 27.8 us)
